TPU v7x, 128 devices: a whole 4x4x4 slice. The times are simulated.
128 devices in a mesh: field: 16 (over x, z), dom: 8 (over y, core).
Axes of the slice: x: 4, y: 4, z: 4, core: 2. Of those that a mesh axis runs over, the one named last changes fastest.
Arguments:
- coefficients: float32 [512, 128], P('dom'), may hold values from -6 to 6
- copies: int32 [512], P('dom'), may hold values from 1 to 4
- owner: int32 [512, 1], P('dom'), may hold values from 0 to 7; in each aligned block of 64 rows (0 to 63, 64 to 127, ...) at most 16 rows name the same one
- snapshots: int32 [8], replicated, may hold values from 0 to 511
- basis: bfloat16 [4194304, 128], P(('field', 'dom')), may hold values from -3 to 3
- observed: float32 [4194304], P(('field', 'dom')), may hold values from -6 to 6
- precision: float32 [4194304], P(('field', 'dom')), may hold values from 1 to 16
Outputs:
- new_coefficients: float32 [8, 8, 16, 128], P('dom')
Inputs may be any that keep to these rules, and one draw needn't show every extreme that they name: Among the 64 particles of one index of dom, at most 16 name the same owner, and in every draw some owner is named by exactly 16 particles of some index of dom.
All inputs are finite; a program needn't handle non-finite values.
Results may differ from a plain program's by a relative error of at most 0.00074.
Values sent between devices are 32-bit elements; how exact they have to be, the bound alone decides.
No kernel may reach another device: no remote copies, remote signals or barrier semaphores. Data moves between devices by JAX's collectives and lax.ppermute only.
A program may use at most 64 MiB of HBM per device.

v0:
```python
import math

import jax
import jax.numpy as jnp
from jax import lax
from jax.sharding import Mesh
from jax.sharding import PartitionSpec as P

PTS = 4194304
DOM = ("dom_0", "dom_1")
FIELD_DOM = ("field_0", "field_1", "dom_0", "dom_1")
FIELD = ("field_0", "field_1")


highest = lax.Precision.HIGHEST
last_pair = (((1,), (1,)), ((), ()))


def in_one_piece(arrays, axis, dim, along):
    columns = [a.reshape(*a.shape[:along], -1) for a in arrays]
    both = jnp.concatenate(columns, axis=along)
    result, at, outs = (lax.all_gather(both, axis, axis=dim, tiled=True), 0, [])
    for a, column in zip(arrays, columns):
        piece = result[..., at : at + column.shape[along]]
        outs.append(piece.reshape(*piece.shape[:along], *a.shape[along:]))
        at += column.shape[along]
    return tuple(outs)


def in_blocks(shard, dim, peers):
    before, after = (shard.shape[:dim], shard.shape[dim + 1 :])
    return jnp.moveaxis(shard.reshape(*before, peers, -1, *after), dim, 0)


def summed_on_arrival(shard, axis, dim):
    peers = lax.axis_size(axis)
    blocks = lax.all_to_all(in_blocks(shard, dim, peers), axis, 0, 0, tiled=True)
    return jnp.sum(blocks, axis=0)


def sum_in_two_steps(shard, axes, dim):
    far, near = axes
    own = summed_on_arrival(in_blocks(shard, dim, lax.axis_size(far)), near, dim + 1)
    return jnp.sum(lax.all_to_all(own, far, 0, 0, tiled=True), axis=0)


def padded_to(lines, peers):
    spare = -lines.shape[0] % peers
    if not spare:
        return lines
    return jnp.concatenate([lines, jnp.zeros((spare, *lines.shape[1:]), lines.dtype)])


def sent_to_all(shard, axis):
    copies = jnp.broadcast_to(shard, (lax.axis_size(axis), *shard.shape))
    return lax.all_to_all(copies, axis, split_axis=0, concat_axis=0, tiled=True)


def laid_out(blocks, dim):
    lengths = list(blocks.shape[1:])
    lengths[dim] *= blocks.shape[0]
    return jnp.moveaxis(blocks, 0, dim).reshape(lengths)


def whole_of(shard, axes, dim):
    far, near = axes
    initial = sent_to_all(shard, far)
    blocks = jnp.swapaxes(sent_to_all(initial, near), 0, 1)
    return laid_out(blocks.reshape(-1, *shard.shape), dim)


def nested_sum(shard, axes):
    own = sum_in_two_steps(
        padded_to(shard, lax.axis_size(axes[0]) * lax.axis_size(axes[1])), axes, 0
    )
    whole = whole_of(own, axes, 0)
    return whole[: len(shard)].reshape(shard.shape)


def together(arrays, axis):
    line, at, outs = (jnp.concatenate([a.reshape(-1) for a in arrays]), 0, [])
    so_far = nested_sum(line, axis)
    for a in arrays:
        outs.append(so_far[at : at + a.size].reshape(a.shape))
        at += a.size
    return tuple(outs)


def collect(shard, axis, dim):
    blocks = sent_to_all(shard, axis)
    return laid_out(blocks, dim)


def pack_rows(updated, owner_column, slot_count, owners):
    labels = owner_column[:, 0]
    onehot = (labels[:, None] == jnp.arange(owners, dtype=jnp.int32)[None, :]).astype(jnp.int32)
    before = jnp.sum(onehot * (jnp.cumsum(onehot, axis=0) - 1), axis=1)
    target = labels * slot_count + before
    placing = (jnp.arange(owners * slot_count, dtype=jnp.int32)[:, None] == target[None, :]).astype(
        jnp.int32
    )
    source = jnp.sum(placing * jnp.arange(updated.shape[0], dtype=jnp.int32)[None, :], axis=1)
    filled = jnp.sum(placing, axis=1) > 0
    packed = jnp.where(filled[:, None], updated[source], jnp.zeros((), jnp.float32))
    return packed.reshape(owners, slot_count, updated.shape[1])


def body(coefficients, copies, owner, snapshots, basis, observed, precision):
    owners = lax.axis_size(DOM)
    block_rows = coefficients.shape[0]
    rank_width = coefficients.shape[1]
    density = rank_width / PTS
    everyone, counts = in_one_piece((coefficients, copies.astype(jnp.float32)), DOM, 0, 1)
    rounded = everyone.astype(jnp.bfloat16)
    total_rows = everyone.shape[0]
    block_width = math.gcd(total_rows, 256)

    def particle_block(block_index):
        particle_part = lax.dynamic_slice_in_dim(rounded, block_index * block_width, block_width, 0)
        field_values = lax.dot_general(
            particle_part, basis, last_pair, preferred_element_type=jnp.float32
        )
        pulled = (density * precision * jnp.tanh(field_values - observed)).astype(jnp.bfloat16)
        return jnp.dot(pulled, basis, preferred_element_type=jnp.float32)

    grad_part = lax.map(particle_block, jnp.arange(total_rows // block_width, dtype=jnp.int32))
    grad_part = grad_part.reshape(total_rows, rank_width)
    picked = rounded[snapshots]
    snap_values = lax.dot_general(picked, basis, last_pair, preferred_element_type=jnp.float32)
    slopes = jnp.tanh(snap_values - observed)
    bending = density * precision * (1.0 - slopes * slopes)

    def snapshot_block(bend_row):
        scaled = (bend_row[:, None] * basis).astype(jnp.bfloat16)
        return lax.dot_general(
            scaled, basis, (((0,), (0,)), ((), ())), preferred_element_type=jnp.float32
        )

    hess_part = lax.map(snapshot_block, bending)
    hess_sum, grad_sum = together(
        (hess_part, grad_part), (("field_0", "field_1", "dom_0"), "dom_1")
    )
    hessians = jnp.eye(rank_width, dtype=jnp.float32)[None] + hess_sum
    mean_hess = jnp.mean(hessians, axis=0)
    hess_trace = jnp.trace(mean_hess)
    repulse = 6.0 / hess_trace
    lifted = jnp.dot(everyone, mean_hess, precision=highest)
    quad_norms = jnp.sum(lifted * everyone, axis=1)
    carried_low = (everyone + repulse * lifted).astype(jnp.bfloat16)
    block_first = lax.axis_index(DOM) * block_rows
    row_count = block_rows // lax.axis_size(FIELD)
    offset = lax.axis_index(FIELD) * row_count
    row_start = block_first + offset
    near_lift = lax.dynamic_slice_in_dim(lifted, row_start, row_count, 0)
    near_norms = lax.dynamic_slice_in_dim(quad_norms, row_start, row_count, 0)
    cross_terms = lax.dot_general(
        near_lift, everyone, last_pair, precision=highest, preferred_element_type=jnp.float32
    )
    distance = near_norms[:, None] + quad_norms[None, :] - 2.0 * cross_terms
    weights = counts[None, :] * jnp.exp(-3.0 * distance / hess_trace)
    weight_total = jnp.sum(weights, axis=1)
    weights_low = weights.astype(jnp.bfloat16)
    own_lift = lax.dynamic_slice_in_dim(lifted, row_start, row_count, 0)
    own_norms = lax.dynamic_slice_in_dim(quad_norms, row_start, row_count, 0)
    numerator = jnp.dot(weights_low, carried_low, preferred_element_type=jnp.float32)
    numerator = numerator + jnp.dot(weights_low.astype(jnp.float32), grad_sum, precision=highest)
    drift_rows = -numerator / weight_total[:, None] + repulse * own_lift
    snap_coef = everyone[snapshots]
    snap_cross = lax.dot_general(
        own_lift, snap_coef, last_pair, precision=highest, preferred_element_type=jnp.float32
    )
    snap_dist = own_norms[:, None] + quad_norms[snapshots][None, :] - 2.0 * snap_cross
    mixture = 1.0 / jnp.square(1.0 + snap_dist / hess_trace)
    mixture = mixture / jnp.sum(mixture, axis=1, keepdims=True)
    local_hess = jnp.einsum("is,srq->irq", mixture, hessians, precision=highest)
    factor = jnp.linalg.cholesky(local_hess)
    halfway = jax.scipy.linalg.solve_triangular(factor, drift_rows[:, :, None], lower=True)
    newton_step = jax.scipy.linalg.solve_triangular(factor, halfway, lower=True, trans=1)
    updated = lax.dynamic_slice_in_dim(everyone, row_start, row_count, 0) + newton_step[:, :, 0]
    updated = collect(updated, FIELD, 0)
    packed = pack_rows(updated, owner, 2 * block_rows // owners, owners)
    arrived = lax.all_to_all(packed, DOM, split_axis=0, concat_axis=0, tiled=True)
    return arrived[None]


def solution(mesh):
    finer = Mesh(mesh.devices.reshape(4, 4, 4, 2), ("field_0", "field_1", "dom_0", "dom_1"))
    return jax.shard_map(
        body,
        mesh=finer,
        in_specs=(
            P(DOM, None),
            P(DOM),
            P(DOM, None),
            P(),
            P(FIELD_DOM, None),
            P(FIELD_DOM),
            P(FIELD_DOM),
        ),
        out_specs=P(DOM, None, None, None),
        check_vma=False,
    )
```

profile of v0, /device:TPU:1, one launch (start us, length us, event | category | flops | bytes accessed | tf_op | source)
XLA Modules:
  0.0 369.9 jit_solution(6363312659181166869)
XLA Ops:
  1.5 15.0 %all_gather.3 = f32[512,129]{1,0:T(8,128)S(1)} all-gather(f32[64,129]{1,0:T(8,128)S(1)} %pad_maximum_fusion.1), channel_id=1, replica_groups=mesh['field_0'=4,'field_1'=4,'dom_0'=4,'dom_1'=2] {'dom_0','dom_1'}, dimensions={0}, use_global_device_ids=true | all-gather | bytes 297216 | tf_op jit(solution)/shard_map/all_gather | solution.py:22
  19.4 5.7 %fusion.17 = f32[8,32768]{1,0:T(8,128)S(1)} fusion(bf16[8,128]{1,0:T(8,128)(2,1)S(1)} %gather_fusion, bf16[32768,128]{1,0:T(8,128)(2,1)} %param.15, f32[32768]{0:T(1024)} %param.16, f32[32768]{0:T(1024)S(1)} %broadcast_multiply_fusion.1), kind=kOutput, calls=%fused_computation.24 | convolution fusion | flops 68157440 | bytes 9701376 | tf_op jit(solution)/shard_map/dot_general | solution.py:129
  25.2 145.2 %while.20 = (s32[]{:T(128)}, f32[8,128,128]{2,1,0:T(8,128)S(1)}, f32[8,32768]{1,0:T(8,128)S(1)}, bf16[32768,128]{1,0:T(8,128)(2,1)}, s32[]{:T(128)}) while((s32[]{:T(128)}, f32[8,128,128]{2,1,0:T(8,128)S(1)}, f32[8,32768]{1,0:T(8,128)S(1)}, bf16[32768,128]{1,0:T(8,128)(2,1)}, s32[]{:T(128)}) %tuple.40), condition=%wide.region_4.5_spmd, body=%wide.region_3.4_spmd.sunk | while | flops 1086324736 | bytes 17236544 | solution.py:139
  25.3 18.0 %fusion.81 = f32[8,128,128]{2,1,0:T(8,128)S(1)} fusion(f32[8,128,128]{2,1,0:T(8,128)S(1)} %get-tuple-element.207, s32[]{:T(128)} %get-tuple-element.206, bf16[32768,128]{1,0:T(8,128)(2,1)} %get-tuple-element.214, f32[32768]{0:T(1024)S(1)} %bitcast.78), kind=kOutput, calls=%fused_computation.8.clone.1 | convolution fusion | flops 1086324736 | bytes 16974336 | tf_op jit(solution)/shard_map/while/body/eval_jaxpr/dot_general | solution.py:135
  43.4 18.0 %fusion.81 = f32[8,128,128]{2,1,0:T(8,128)S(1)} fusion(f32[8,128,128]{2,1,0:T(8,128)S(1)} %get-tuple-element.207, s32[]{:T(128)} %get-tuple-element.206, bf16[32768,128]{1,0:T(8,128)(2,1)} %get-tuple-element.214, f32[32768]{0:T(1024)S(1)} %bitcast.78), kind=kOutput, calls=%fused_computation.8.clone.1 | convolution fusion | flops 1086324736 | bytes 16974336 | tf_op jit(solution)/shard_map/while/body/eval_jaxpr/dot_general | solution.py:135
  61.6 18.0 %fusion.81 = f32[8,128,128]{2,1,0:T(8,128)S(1)} fusion(f32[8,128,128]{2,1,0:T(8,128)S(1)} %get-tuple-element.207, s32[]{:T(128)} %get-tuple-element.206, bf16[32768,128]{1,0:T(8,128)(2,1)} %get-tuple-element.214, f32[32768]{0:T(1024)S(1)} %bitcast.78), kind=kOutput, calls=%fused_computation.8.clone.1 | convolution fusion | flops 1086324736 | bytes 16974336 | tf_op jit(solution)/shard_map/while/body/eval_jaxpr/dot_general | solution.py:135
  79.7 18.0 %fusion.81 = f32[8,128,128]{2,1,0:T(8,128)S(1)} fusion(f32[8,128,128]{2,1,0:T(8,128)S(1)} %get-tuple-element.207, s32[]{:T(128)} %get-tuple-element.206, bf16[32768,128]{1,0:T(8,128)(2,1)} %get-tuple-element.214, f32[32768]{0:T(1024)S(1)} %bitcast.78), kind=kOutput, calls=%fused_computation.8.clone.1 | convolution fusion | flops 1086324736 | bytes 16974336 | tf_op jit(solution)/shard_map/while/body/eval_jaxpr/dot_general | solution.py:135
  97.9 18.0 %fusion.81 = f32[8,128,128]{2,1,0:T(8,128)S(1)} fusion(f32[8,128,128]{2,1,0:T(8,128)S(1)} %get-tuple-element.207, s32[]{:T(128)} %get-tuple-element.206, bf16[32768,128]{1,0:T(8,128)(2,1)} %get-tuple-element.214, f32[32768]{0:T(1024)S(1)} %bitcast.78), kind=kOutput, calls=%fused_computation.8.clone.1 | convolution fusion | flops 1086324736 | bytes 16974336 | tf_op jit(solution)/shard_map/while/body/eval_jaxpr/dot_general | solution.py:135
  116.0 18.0 %fusion.81 = f32[8,128,128]{2,1,0:T(8,128)S(1)} fusion(f32[8,128,128]{2,1,0:T(8,128)S(1)} %get-tuple-element.207, s32[]{:T(128)} %get-tuple-element.206, bf16[32768,128]{1,0:T(8,128)(2,1)} %get-tuple-element.214, f32[32768]{0:T(1024)S(1)} %bitcast.78), kind=kOutput, calls=%fused_computation.8.clone.1 | convolution fusion | flops 1086324736 | bytes 16974336 | tf_op jit(solution)/shard_map/while/body/eval_jaxpr/dot_general | solution.py:135
  134.2 18.0 %fusion.81 = f32[8,128,128]{2,1,0:T(8,128)S(1)} fusion(f32[8,128,128]{2,1,0:T(8,128)S(1)} %get-tuple-element.207, s32[]{:T(128)} %get-tuple-element.206, bf16[32768,128]{1,0:T(8,128)(2,1)} %get-tuple-element.214, f32[32768]{0:T(1024)S(1)} %bitcast.78), kind=kOutput, calls=%fused_computation.8.clone.1 | convolution fusion | flops 1086324736 | bytes 16974336 | tf_op jit(solution)/shard_map/while/body/eval_jaxpr/dot_general | solution.py:135
  152.3 18.0 %fusion.81 = f32[8,128,128]{2,1,0:T(8,128)S(1)} fusion(f32[8,128,128]{2,1,0:T(8,128)S(1)} %get-tuple-element.207, s32[]{:T(128)} %get-tuple-element.206, bf16[32768,128]{1,0:T(8,128)(2,1)} %get-tuple-element.214, f32[32768]{0:T(1024)S(1)} %bitcast.78), kind=kOutput, calls=%fused_computation.8.clone.1 | convolution fusion | flops 1086324736 | bytes 16974336 | tf_op jit(solution)/shard_map/while/body/eval_jaxpr/dot_general | solution.py:135
  170.4 32.2 %while.21 = (s32[]{:T(128)}, f32[2,256,128]{2,1,0:T(8,128)S(1)}, f32[32768]{0:T(1024)S(1)}, s32[2]{0:T(128)S(1)}, bf16[512,128]{1,0:T(8,128)(2,1)S(1)}, /*index=...) while((s32[]{:T(128)}, f32[2,256,128]{2,1,0:T(8,128)S(1)}, ...), condition=%wide.region_6.7_spmd, body=%wide.region_5.6_spmd.sunk | while | flops 4320165888 | bytes 17498796 | solution.py:126
  171.6 14.9 %fusion.85 = f32[2,256,128]{2,1,0:T(8,128)S(1)} fusion(f32[2,256,128]{2,1,0:T(8,128)S(1)} %get-tuple-element.180, s32[]{:T(128)} %get-tuple-element.179, bf16[32768,128]{1,0:T(8,128)(2,1)} %get-tuple-element.195, f32[32768]{0:T(1024)S(1)} %get-tuple-element.196, f32[32768]{0:T(1024)S(1)} %broadcast_multiply_fusion.3, ...), kind=kOutput, calls=%fused_computation.16.clone.1 | convolution fusion | flops 4320133120 | bytes 17236484 | tf_op jit(solution)/shard_map/while/body/eval_jaxpr/dot_general | solution.py:124
  187.7 14.9 %fusion.85 = f32[2,256,128]{2,1,0:T(8,128)S(1)} fusion(f32[2,256,128]{2,1,0:T(8,128)S(1)} %get-tuple-element.180, s32[]{:T(128)} %get-tuple-element.179, bf16[32768,128]{1,0:T(8,128)(2,1)} %get-tuple-element.195, f32[32768]{0:T(1024)S(1)} %get-tuple-element.196, f32[32768]{0:T(1024)S(1)} %broadcast_multiply_fusion.3, ...), kind=kOutput, calls=%fused_computation.16.clone.1 | convolution fusion | flops 4320133120 | bytes 17236484 | tf_op jit(solution)/shard_map/while/body/eval_jaxpr/dot_general | solution.py:124
  203.2 4.2 %all_to_all.38 = f32[2,64,1536]{2,1,0:T(8,128)S(1)} all-to-all(f32[2,64,1536]{2,1,0:T(8,128)S(1)} %copy.29), channel_id=1, replica_groups=mesh['field_0'=4,'field_1'=4,'dom_0'=4,'dom_1'=2] {'dom_1'}, dimensions={0} | all-to-all | bytes 1572864 | tf_op jit(solution)/shard_map/all_to_all | solution.py:37
  208.5 10.6 %all-to-all-start.1 = ((f32[64,1,1536]{2,1,0:T(1,128)}), f32[64,1,1536]{2,1,0:T(1,128)S(1)}, u32[]{:S(2)}, u32[]{:S(2)}) async-start(f32[64,1,1536]{2,1,0:T(1,128)} %all_to_all.25), calls=%async_computation.1 | async-start | bytes 786432 | tf_op jit(solution)/shard_map/all_to_all | solution.py:44
  219.6 10.1 %all-to-all-done.1 = f32[64,1,1536]{2,1,0:T(1,128)S(1)} async-done(((f32[64,1,1536]{2,1,0:T(1,128)}), f32[64,1,1536]{2,1,0:T(1,128)S(1)}, u32[]{:S(2)}, u32[]{:S(2)}) %all-to-all-start.1) | async-done | bytes 393248 | tf_op jit(solution)/shard_map/all_to_all | solution.py:44
  230.9 4.8 %all-to-all-start.2 = ((f32[64,1,1536]{2,1,0:T(1,128)}), f32[64,1,1536]{2,1,0:T(1,128)S(1)}, u32[]{:S(2)}, u32[]{:S(2)}) async-start(f32[64,1,1536]{2,1,0:T(1,128)} %broadcast_in_dim.74), calls=%async_computation.2 | async-start | bytes 786432 | tf_op jit(solution)/shard_map/all_to_all | solution.py:56
  235.9 9.8 %all-to-all-done.2 = f32[64,1,1536]{2,1,0:T(1,128)S(1)} async-done(((f32[64,1,1536]{2,1,0:T(1,128)}), f32[64,1,1536]{2,1,0:T(1,128)S(1)}, u32[]{:S(2)}, u32[]{:S(2)}) %all-to-all-start.2) | async-done | bytes 393248 | tf_op jit(solution)/shard_map/all_to_all | solution.py:56
  245.8 7.2 %all_to_all.39 = f32[2,64,1536]{2,1,0:T(8,128)S(1)} all-to-all(f32[2,64,1536]{2,1,0:T(8,128)S(1)} %broadcast_in_dim.75), channel_id=1, replica_groups=mesh['field_0'=4,'field_1'=4,'dom_0'=4,'dom_1'=2] {'dom_1'}, dimensions={0} | all-to-all | bytes 1572864 | tf_op jit(solution)/shard_map/all_to_all | solution.py:56
  259.6 46.9 %custom-call.11 = f32[4,128,128]{2,1,0:T(8,128)S(1)} custom-call(f32[4,128,128]{2,1,0:T(8,128)S(1)} %fusion.36), custom_call_target="Cholesky" | custom-call | tf_op jit(solution)/shard_map/jit(cholesky)/cholesky | solution.py:176
  306.8 39.3 %custom-call.12 = f32[4,1,128,128]{2,3,1,0:T(8,128)S(1)} custom-call(f32[4,1,128,128]{3,2,1,0:T(8,128)S(1)} %select_bitcast_fusion), custom_call_target="InvertDiagBlocksLowerTriangular" | custom-call | tf_op jit(solution)/shard_map/jit(_solve_triangular)/vmap()/triangular_solve | solution.py:178
  353.5 6.3 %all-to-all-done.4 = f32[16,4,128]{2,1,0:T(4,128)S(1)} async-done(((f32[16,4,128]{2,1,0:T(4,128)}), f32[16,4,128]{2,1,0:T(4,128)S(1)}, u32[]{:S(2)}, u32[]{:S(2)}) %all-to-all-start.4) | async-done | bytes 32800 | tf_op jit(solution)/shard_map/all_to_all | solution.py:56
  360.5 8.7 %all_to_all.40 = f32[8,16,128]{2,1,0:T(8,128)S(1)} all-to-all(f32[8,16,128]{2,1,0:T(8,128)S(1)} %broadcast_select_fusion), channel_id=1, replica_groups=mesh['field_0'=4,'field_1'=4,'dom_0'=4,'dom_1'=2] {'dom_0','dom_1'}, dimensions={0} | all-to-all | bytes 131072 | tf_op jit(solution)/shard_map/all_to_all | solution.py:182
  (85 shorter events, 24.9 us)
Async XLA Ops:
  16.5 0.8 copy-start
  18.0 7.2 %copy-start.4 = (s32[1024]{0:T(1024)}, s32[1024]{0:T(1024)S(1)}, u32[]{:S(2)}) copy-start(s32[1024]{0:T(1024)S(1)} %pad_clamp_fusion.1) | copy-start | bytes 12292
  25.1 145.2 %copy-start.2 = (f32[32768]{0:T(1024)S(1)}, f32[32768]{0:T(1024)}, u32[]{:S(2)}) copy-start(f32[32768]{0:T(1024)} %param.17) | copy-start | bytes 393220
  25.1 145.2 %copy-start.3 = (f32[32768]{0:T(1024)S(1)}, f32[32768]{0:T(1024)}, u32[]{:S(2)}) copy-start(f32[32768]{0:T(1024)} %param.16) | copy-start | bytes 393220
  202.6 16.5 %copy-start.5 = (s32[64,1]{0,1:T(1,128)S(1)}, s32[64,1]{0,1:T(1,128)}, u32[]{:S(2)}) copy-start(s32[64,1]{0,1:T(1,128)} %param.13) | copy-start | bytes 772
  202.6 33.1 %copy-start.1 = (f32[512,129]{1,0:T(8,128)S(1)}, f32[512,129]{1,0:T(8,128)}, u32[]{:S(2)}) copy-start(f32[512,129]{1,0:T(8,128)} %copy-done) | copy-start | bytes 792580
  208.5 21.2 %all-to-all-start.1 = ((f32[64,1,1536]{2,1,0:T(1,128)}), f32[64,1,1536]{2,1,0:T(1,128)S(1)}, u32[]{:S(2)}, u32[]{:S(2)}) async-start(f32[64,1,1536]{2,1,0:T(1,128)} %all_to_all.25), calls=%async_computation.1 | async-start | bytes 786432 | tf_op jit(solution)/shard_map/all_to_all | solution.py:44
  230.9 14.8 %all-to-all-start.2 = ((f32[64,1,1536]{2,1,0:T(1,128)}), f32[64,1,1536]{2,1,0:T(1,128)S(1)}, u32[]{:S(2)}, u32[]{:S(2)}) async-start(f32[64,1,1536]{2,1,0:T(1,128)} %broadcast_in_dim.74), calls=%async_computation.2 | async-start | bytes 786432 | tf_op jit(solution)/shard_map/all_to_all | solution.py:56
  349.9 9.9 %all-to-all-start.4 = ((f32[16,4,128]{2,1,0:T(4,128)}), f32[16,4,128]{2,1,0:T(4,128)S(1)}, u32[]{:S(2)}, u32[]{:S(2)}) async-start(f32[16,4,128]{2,1,0:T(4,128)} %broadcast_in_dim.77), calls=%async_computation.4 | async-start | bytes 65536 | tf_op jit(solution)/shard_map/all_to_all | solution.py:56
where the time goes:
time: 370 us
  matrix products  184 us (50%)
  other arithmetic  91.4 us (25%)
  blocking collectives  35 us (9%)
  waiting for transfers between devices  26.2 us (7%)
  starting transfers between devices  18.9 us (5%)
  local copies, waits for them, and re-layouts  11.7 us (3%)
    dot_general x8, matrix products, snapshot_block(): lax.dot_general(scaled, basis, (((0,), (0,)), ((), ())), preferred_elemen...  144 us
    another operation x4, other arithmetic, body(): factor = jnp.linalg.cholesky(local_hess)  47.1 us
    another operation x3, other arithmetic, body(): jax.scipy.linalg.solve_triangular(factor, halfway, lower=True, trans=1)  39.4 us
    dot_general x2, matrix products, particle_block(): return jnp.dot(pulled, basis, preferred_element_type=jnp.float32)  29.8 us
    all_to_all x2, waiting for transfers between devices, sent_to_all(): return lax.all_to_all(copies, axis, split_axis=0, concat_axis=0, tiled=True)  16.1 us
    all_gather x1, blocking collectives, in_one_piece(): result, at, outs = (lax.all_gather(both, axis, axis=dim, tiled=True), 0, [])  15 us
    all_to_all x1, starting transfers between devices, sum_in_two_steps(): return jnp.sum(lax.all_to_all(own, far, 0, 0, tiled=True), axis=0)  10.6 us
    all_to_all x1, waiting for transfers between devices, sum_in_two_steps(): return jnp.sum(lax.all_to_all(own, far, 0, 0, tiled=True), axis=0)  10.1 us
  transfers between devices with their start and end apart: 3, of which 3 were waited for; matrix products, arithmetic and copies ran while one was open for 0% of the time, Pallas kernels for 0%

commit v1 on v0

v1 whole, which is shorter than its diff:
```python
import functools

import jax
import jax.numpy as jnp
from jax import lax
from jax.experimental import pallas as pl
from jax.experimental.pallas import tpu as pltpu
from jax.sharding import Mesh
from jax.sharding import PartitionSpec as P

PTS = 4194304
R = 128
NP_DEV = 64
NPART = 512
SNAP = 8
N_DOM = 8
ROWS = NPART + SNAP * R
HALF = ROWS // 2
LINES = 72
X, Z, Y, C = "field_0", "field_1", "dom_0", "dom_1"
DOM = (Y, C)
FIELD = (X, Z)
CHIPS = (X, Z, Y)
FIELD_DOM = (X, Z, Y, C)
f32, bf16 = jnp.float32, jnp.bfloat16
highest = lax.Precision.HIGHEST
last_pair = (((1,), (1,)), ((), ()))
VMEM_LIMIT = 60 << 20


def particles(gathered_ref):
    return jnp.concatenate([gathered_ref[d, 0:NP_DEV, :] for d in range(N_DOM)], axis=0)


def points_kernel(block, chunk, picks_ref, core_ref, gathered_ref, obs_ref, prec_ref, basis_ref,
                  keep_ref, send_ref, coef_ref, sums_ref, left_ref, right_ref):
    step = pl.program_id(0)

    @pl.when(step == 0)
    def _():
        sums_ref[...] = jnp.zeros_like(sums_ref)
        coef_ref[0:NPART, :] = particles(gathered_ref).astype(bf16)
        rows = []
        for s in range(SNAP):
            j = picks_ref[s]
            rows.append(gathered_ref[j // NP_DEV, pl.ds(j % NP_DEV, 1), :])
        rows.append(jnp.zeros((SNAP, R), f32))
        coef_ref[NPART : NPART + 16, :] = jnp.concatenate(rows, axis=0).astype(bf16)

    for c in range(block // chunk):
        at = pl.ds(c * chunk, chunk)
        rows = basis_ref[at, :]
        columns = rows.T
        prec = prec_ref[:, at]
        right_ref[at, :] = (columns.astype(f32) * prec).astype(bf16).T
        field = lax.dot_general(coef_ref[...], rows, last_pair, preferred_element_type=f32)
        slopes = jnp.tanh(field[: NPART + SNAP] - obs_ref[:, at])
        left_ref[0:NPART, at] = slopes[:NPART].astype(bf16)
        picked = slopes[NPART : NPART + SNAP]
        bend = 1.0 - picked * picked
        for s in range(SNAP):
            top = NPART + s * R
            left_ref[top : top + R, at] = bend[s : s + 1, :].astype(bf16) * columns
    sums_ref[...] += jnp.dot(left_ref[...], right_ref[...], preferred_element_type=f32)

    @pl.when(step == pl.num_programs(0) - 1)
    def _():
        for core in range(2):

            @pl.when(core_ref[0] == core)
            def _():
                keep_ref[...] = sums_ref[core * HALF : (core + 1) * HALF, :]
                send_ref[...] = sums_ref[(1 - core) * HALF : (2 - core) * HALF, :]


def points_pass(snapshots, core, gathered, observed, precision, basis):
    block, chunk = 2048, 256
    count = basis.shape[0]
    whole = lambda i, *_: (0, 0)
    return pl.pallas_call(
        functools.partial(points_kernel, block, chunk),
        out_shape=[jax.ShapeDtypeStruct((HALF, R), f32)] * 2,
        grid_spec=pltpu.PrefetchScalarGridSpec(
            num_scalar_prefetch=2,
            grid=(count // block,),
            in_specs=[
                pl.BlockSpec((N_DOM, LINES, R), lambda i, *_: (0, 0, 0)),
                pl.BlockSpec((1, block), lambda i, *_: (0, i)),
                pl.BlockSpec((1, block), lambda i, *_: (0, i)),
                pl.BlockSpec((block, R), lambda i, *_: (i, 0)),
            ],
            out_specs=[pl.BlockSpec((HALF, R), whole)] * 2,
            scratch_shapes=[
                pltpu.VMEM((NPART + 16, R), bf16),
                pltpu.VMEM((ROWS, R), f32),
                pltpu.VMEM((ROWS, block), bf16),
                pltpu.VMEM((block, R), bf16),
            ],
        ),
        compiler_params=pltpu.CompilerParams(vmem_limit_bytes=VMEM_LIMIT),
        name="points_pass",
    )(snapshots, core, gathered, observed.reshape(1, count), precision.reshape(1, count), basis)


def lane_of(rows, k):
    return jnp.take_along_axis(rows, jnp.full(rows.shape, k, jnp.int32), axis=1)


def steps_kernel(where_ref, picks_ref, gathered_ref, mine_ref, other_ref, out_ref,
                 sums_ref, sys_ref):
    scale = R / PTS
    core, dom, source, first = where_ref[0], where_ref[1], where_ref[2], where_ref[3]
    for half in range(2):

        @pl.when(core == half)
        def _():
            sums_ref[half * HALF : (half + 1) * HALF, :] = mine_ref[...]
            sums_ref[(1 - half) * HALF : (2 - half) * HALF, :] = other_ref[...]

    lane = lax.broadcasted_iota(jnp.int32, (8, R), 1)
    sub = lax.broadcasted_iota(jnp.int32, (8, R), 0)
    square_r = lax.broadcasted_iota(jnp.int32, (R, R), 0)
    square_q = lax.broadcasted_iota(jnp.int32, (R, R), 1)
    eye = (square_r == square_q).astype(f32)

    everyone = particles(gathered_ref)
    tags = [gathered_ref[d, NP_DEV : NP_DEV + 1, :] for d in range(N_DOM)]
    low = lane[0:1] < NP_DEV
    counts = jnp.concatenate(
        [jnp.where(low, tags[d], pltpu.roll(tags[d + 1], NP_DEV, 1)) for d in range(0, N_DOM, 2)], axis=1
    )

    owners = pltpu.roll(jnp.broadcast_to(gathered_ref[source, NP_DEV : NP_DEV + 1, :], (8, R)), NP_DEV, 1)
    named = jnp.where((owners == dom.astype(f32)) & (lane < NP_DEV), 1.0, 0.0)
    before = jnp.dot(named, (square_r < square_q).astype(f32), precision=highest, preferred_element_type=f32)
    slot = (sub + first).astype(f32)
    choose = jnp.where((named > 0.5) & (before == slot), 1.0, 0.0)
    valid = jnp.sum(choose, axis=1, keepdims=True)
    own = jnp.dot(choose[:, :NP_DEV], gathered_ref[source, 0:NP_DEV, :], precision=highest,
                  preferred_element_type=f32)

    mean_hess = sums_ref[NPART : NPART + R, :]
    for s in range(1, SNAP):
        mean_hess = mean_hess + sums_ref[NPART + s * R : NPART + (s + 1) * R, :]
    mean_hess = eye + mean_hess * (scale / SNAP)
    trace = jnp.sum(jnp.sum(mean_hess * eye, axis=1, keepdims=True), axis=0, keepdims=True)
    repulse = 6.0 / trace

    lifted = jnp.dot(everyone, mean_hess, precision=highest, preferred_element_type=f32)
    ones = jnp.ones((8, R), f32)
    norms = lax.dot_general(ones, lifted * everyone, last_pair, precision=highest, preferred_element_type=f32)
    own_lift = jnp.dot(own, mean_hess, precision=highest, preferred_element_type=f32)
    own_norm = jnp.sum(own_lift * own, axis=1, keepdims=True)
    cross = lax.dot_general(own_lift, everyone, last_pair, precision=highest, preferred_element_type=f32)
    distance = own_norm + norms - 2.0 * cross
    weights = counts * jnp.exp(-3.0 * distance / trace)
    total = jnp.sum(weights, axis=1, keepdims=True)
    low_weights = weights.astype(bf16)
    carried = (everyone + repulse * lifted).astype(bf16)
    numerator = jnp.dot(low_weights, carried, preferred_element_type=f32)
    grad = jnp.dot(low_weights.astype(f32), sums_ref[0:NPART, :], precision=highest, preferred_element_type=f32)
    drift = -(numerator + scale * grad) / total + repulse * own_lift

    rows = []
    for s in range(SNAP):
        j = picks_ref[s]
        rows.append(gathered_ref[j // NP_DEV, pl.ds(j % NP_DEV, 1), :])
    rows.append(jnp.zeros((R - SNAP, R), f32))
    picked = jnp.concatenate(rows, axis=0)
    picked_lift = jnp.dot(picked, mean_hess, precision=highest, preferred_element_type=f32)
    picked_norm = lax.dot_general(ones, picked_lift * picked, last_pair, precision=highest,
                                  preferred_element_type=f32)
    picked_cross = lax.dot_general(own_lift, picked, last_pair, precision=highest, preferred_element_type=f32)
    apart = 1.0 + (own_norm + picked_norm - 2.0 * picked_cross) / trace
    mixture = jnp.where(lane < SNAP, 1.0 / (apart * apart), 0.0)
    mixture = mixture / jnp.sum(mixture, axis=1, keepdims=True)

    shares = [jnp.broadcast_to(mixture[:, s : s + 1], (8, R)) for s in range(SNAP)]
    share_sum = functools.reduce(jnp.add, shares)
    shares = [share * scale for share in shares]

    def assemble(g, carry):
        tiles = [sums_ref[pl.ds(pl.multiple_of(NPART + s * R + g * 8, 8), 8), :] for s in range(SNAP)]
        for k in range(8):
            row = jnp.where(lane == g * 8 + k, share_sum, 0.0)
            for s in range(SNAP):
                row = row + shares[s] * tiles[s][k : k + 1, :]
            sys_ref[g * 8 + k] = row
        return carry

    lax.fori_loop(0, R // 8, assemble, 0)

    def eliminate(start, h, carry):
        rhs, inverses = carry
        k = start + 2 * h
        r0 = sys_ref[k]
        i0 = 1.0 / lane_of(r0, k)
        s0 = jnp.where(lane > k, r0, 0.0) * i0
        r1 = sys_ref[k + 1] - lane_of(r0, k + 1) * s0
        sys_ref[k + 1] = r1
        i1 = 1.0 / lane_of(r1, k + 1)
        m0 = jnp.where(lane > k + 1, r0, 0.0)
        m1 = jnp.where(lane > k + 1, r1, 0.0)
        s1 = m1 * i1
        rhs = rhs - lane_of(rhs, k) * s0
        rhs = rhs - lane_of(rhs, k + 1) * s1
        inverses = jnp.where(lane == k, i0, jnp.where(lane == k + 1, i1, inverses))
        for i in range(start, R):
            sys_ref[i] = sys_ref[i] - m0[:, i : i + 1] * s0 - m1[:, i : i + 1] * s1
        return rhs, inverses

    carry = (drift, jnp.zeros((8, R), f32))
    segment = R // 4
    for start in range(0, R, segment):
        carry = lax.fori_loop(0, segment // 2, functools.partial(eliminate, start), carry)
    rhs, inverses = carry

    def substitute(n, rhs):
        m = R - 1 - n
        x = lane_of(rhs * inverses, m)
        return rhs - jnp.where(lane < m, sys_ref[m], 0.0) * x

    rhs = lax.fori_loop(0, R, substitute, rhs, unroll=8)
    out_ref[...] = jnp.where(valid > 0.5, own + rhs * inverses, 0.0)


def newton_rows(where, snapshots, gathered, mine, other):
    vmem = pl.BlockSpec(memory_space=pltpu.VMEM)
    smem = pl.BlockSpec(memory_space=pltpu.SMEM)
    return pl.pallas_call(
        steps_kernel,
        out_shape=jax.ShapeDtypeStruct((8, R), f32),
        in_specs=[smem, smem, vmem, vmem, vmem],
        out_specs=vmem,
        scratch_shapes=[pltpu.VMEM((ROWS, R), f32), pltpu.VMEM((R, 8, R), f32)],
        compiler_params=pltpu.CompilerParams(vmem_limit_bytes=VMEM_LIMIT),
        name="newton_rows",
    )(where, snapshots, gathered, mine, other)


def sent_to_all(shard, axes):
    copies = jnp.broadcast_to(shard, (lax.axis_size(axes), *shard.shape))
    return lax.all_to_all(copies, axes, split_axis=0, concat_axis=0, tiled=True)


def body(coefficients, copies, owner, snapshots, basis, observed, precision):
    tags = jnp.concatenate([copies, owner[:, 0]]).astype(f32)[None]
    lines = jnp.concatenate([coefficients, tags, jnp.zeros((LINES - NP_DEV - 1, R), f32)], axis=0)
    gathered = sent_to_all(lines, DOM)
    core = lax.axis_index(C)
    swap = [(0, 1), (1, 0)]
    keep, send = points_pass(snapshots, core.reshape(1), gathered, observed, precision, basis)
    part = keep + lax.ppermute(send, C, swap)
    chips = lax.axis_size(CHIPS)
    blocks = lax.all_to_all(part.reshape(chips, HALF // chips, R), CHIPS, 0, 0, tiled=True)
    mine = sent_to_all(jnp.sum(blocks, axis=0), CHIPS).reshape(HALF, R)
    other = lax.ppermute(mine, C, swap)
    seat = lax.axis_index(FIELD)
    where = jnp.stack([core, lax.axis_index(DOM), seat // 2, seat % 2 * 8])
    rows = newton_rows(where, snapshots, gathered, mine, other)
    return sent_to_all(rows, FIELD).reshape(1, N_DOM, 16, R)


def solution(mesh):
    finer = Mesh(mesh.devices.reshape(4, 4, 4, 2), FIELD_DOM)
    return jax.shard_map(
        body,
        mesh=finer,
        in_specs=(
            P(DOM, None),
            P(DOM),
            P(DOM, None),
            P(),
            P(FIELD_DOM, None),
            P(FIELD_DOM),
            P(FIELD_DOM),
        ),
        out_specs=P(DOM, None, None, None),
        check_vma=False,
    )
```

time: 370 us -> 153 us (0.41)
  matrix products: 184 us -> 0 us
  other arithmetic: 91.4 us -> 3.31 us
  Pallas kernels: 0 us -> 79.5 us
  waiting for transfers between devices: 26.2 us -> 9.12 us
  blocking collectives: 35 us -> 45.7 us
  starting transfers between devices: 18.9 us -> 10.4 us
  local copies, waits for them, and re-layouts: 11.7 us -> 3.7 us
    dot_general x17 -> x0, matrix products: 183 us -> none  [the longest x8 144 us: snapshot_block(): lax.dot_general(scaled, basis, (((0,), (0,)), ((), ())), preferred_elemen...]
    another operation x8 -> x1, other arithmetic: 86.6 us -> 0.6 us  [body(): where = jnp.stack([core, lax.axis_index(DOM), seat // 2, seat % 2 * 8])]
    pallas_call x0 -> x2, Pallas kernels: none -> 79.5 us  [the longest x1 41.7 us: points_pass(): pl.pallas_call(functools.partial(points_kernel, block, chunk), out_shape=...]
    all_to_all x3, blocking collectives: 20.1 us -> 45.7 us  [the longest x2 24.8 us: sent_to_all(): return lax.all_to_all(copies, axes, split_axis=0, concat_axis=0, tiled=True)]
    all_to_all x3 -> x1, waiting for transfers between devices: 26.2 us -> 6.81 us  [sent_to_all(): return lax.all_to_all(copies, axes, split_axis=0, concat_axis=0, tiled=True)]
    all_gather x1 -> x0, blocking collectives: 15 us -> none  [in_one_piece(): result, at, outs = (lax.all_gather(both, axis, axis=dim, tiled=True), 0, [])]
    all_to_all x3 -> x1, starting transfers between devices: 18.9 us -> 5.97 us  [sent_to_all(): return lax.all_to_all(copies, axes, split_axis=0, concat_axis=0, tiled=True)]
    ppermute x0 -> x2, starting transfers between devices: none -> 4.41 us  [the longest x1 3.32 us: body(): other = lax.ppermute(mine, C, swap)]
where the time goes in v1:
time: 153 us; the launch traced here: 152 us
  Pallas kernels  79.5 us (52%)
  blocking collectives  45.7 us (30%)
  starting transfers between devices  10.4 us (7%)
  waiting for transfers between devices  9.12 us (6%)
  local copies, waits for them, and re-layouts  3.7 us (2%)
  other arithmetic  3.31 us (2%)
    pallas_call x1, Pallas kernels, points_pass(): pl.pallas_call(functools.partial(points_kernel, block, chunk), out_shape=...  41.7 us
    pallas_call x1, Pallas kernels, newton_rows(): pl.pallas_call(steps_kernel, out_shape=jax.ShapeDtypeStruct((8, R), f32),...  37.8 us
    all_to_all x2, blocking collectives, sent_to_all(): return lax.all_to_all(copies, axes, split_axis=0, concat_axis=0, tiled=True)  24.8 us
    all_to_all x1, blocking collectives, body(): lax.all_to_all(part.reshape(chips, HALF // chips, R), CHIPS, 0, 0, tiled=...  20.9 us
    all_to_all x1, waiting for transfers between devices, sent_to_all(): return lax.all_to_all(copies, axes, split_axis=0, concat_axis=0, tiled=True)  6.81 us
    all_to_all x1, starting transfers between devices, sent_to_all(): return lax.all_to_all(copies, axes, split_axis=0, concat_axis=0, tiled=True)  5.97 us
    ppermute x1, starting transfers between devices, body(): other = lax.ppermute(mine, C, swap)  3.32 us
  transfers between devices with their start and end apart: 3, of which 3 were waited for; matrix products, arithmetic and copies ran while one was open for 0% of the time, Pallas kernels for 0%

profile of v1, /device:TPU:1, one launch (start us, length us, event | category | flops | bytes accessed | tf_op | source)
XLA Modules:
  0.0 151.7 jit_solution(10734900808573039761)
XLA Ops:
  0.0 0.7 add_convert_fusion
  0.7 0.1 pad.2.clone
  0.8 0.8 maximum_maximum_fusion
  1.7 0.7 broadcast_in_dim.14
  2.4 6.0 %all-to-all-start = ((f32[8,72,128]{2,1,0:T(8,128)}), f32[8,72,128]{2,1,0:T(8,128)S(1)}, u32[]{:S(2)}, u32[]{:S(2)}) async-start(f32[8,72,128]{2,1,0:T(8,128)} %broadcast_in_dim.14), calls=%async_computation | async-start | bytes 589824 | tf_op jit(solution)/shard_map/all_to_all | solution.py:243
  8.4 6.8 %all-to-all-done.gathered_ref = f32[8,72,128]{2,1,0:T(8,128)S(1)} async-done(((f32[8,72,128]{2,1,0:T(8,128)}), f32[8,72,128]{2,1,0:T(8,128)S(1)}, u32[]{:S(2)}, u32[]{:S(2)}) %all-to-all-start) | async-done | bytes 294944 | tf_op jit(solution)/shard_map/all_to_all | solution.py:243
  15.2 0.7 copy-done
  15.9 41.7 %points_pass.1 = (f32[768,128]{1,0:T(8,128)}, f32[768,128]{1,0:T(8,128)}) custom-call(s32[8]{0:T(128)} %picks_ref.3, s32[1]{0:T(128)} %bitcast.core_ref, f32[8,72,128]{2,1,0:T(8,128)} %copy-done, f32[1,32768]{1,0:T(1,128)} %bitcast.10, f32[1,32768]{1,0:T(1,128)} %bitcast.11, bf16[32768,128]{1,0:T(8,128)(2,1)} %basis_ref.1), custom_call_target="tpu_custom_call" | custom-call | tf_op jit(solution)/shard_map/points_pass/pallas_call | solution.py:80
  57.6 1.1 collective-permute-start
  58.7 1.6 %collective-permute-done = f32[768,128]{1,0:T(8,128)S(1)} collective-permute-done((f32[768,128]{1,0:T(8,128)}, f32[768,128]{1,0:T(8,128)S(1)}, u32[]{:S(2)}, u32[]{:S(2)}) %collective-permute-start) | collective-permute-done | bytes 393248 | tf_op jit(solution)/shard_map/ppermute | solution.py:253
  60.2 1.1 add.17
  61.3 20.9 %all_to_all.20 = f32[64,12,128]{2,1,0:T(8,128)S(1)} all-to-all(f32[64,12,128]{2,1,0:T(8,128)S(1)} %reshape.48), channel_id=1, replica_groups=mesh['field_0'=4,'field_1'=4,'dom_0'=4,'dom_1'=2] {'field_0','field_1','..., dimensions={0} | all-to-all | bytes 786432 | tf_op jit(solution)/shard_map/all_to_all | solution.py:255
  82.2 0.1 reduce_sum.9
  82.3 15.5 %all_to_all.21 = f32[64,12,128]{2,1,0:T(8,128)S(1)} all-to-all(f32[64,12,128]{2,1,0:T(8,128)S(1)} %broadcast_in_dim.15), channel_id=1, replica_groups=mesh['field_0'=4,'field_1'=4,'dom_0'=4,'dom_1'=2] {'field_0','field_1','..., dimensions={0} | all-to-all | bytes 786432 | tf_op jit(solution)/shard_map/all_to_all | solution.py:243
  97.9 0.0 copy-start.1
  97.9 3.3 %collective-permute-start.1 = (f32[768,128]{1,0:T(8,128)S(1)}, f32[768,128]{1,0:T(8,128)S(1)}, u32[]{:S(2)}, u32[]{:S(2)}) collective-permute-start(f32[768,128]{1,0:T(8,128)S(1)} %reshape.49.mine_ref), channel_id=1, source_target_pairs={{0,1},{1,0},{2,3},{3,2},{4,5},{5,4},{6,7},{7,6},{8,9},{9,8},{10,11... | collective-permute-start | bytes 1179656 | tf_op jit(solution)/shard_map/ppermute | solution.py:257
  101.2 0.6 pad_add_fusion.where_ref
  101.8 0.7 collective-permute-done.1.other_ref
  102.6 0.0 copy-done.1
  102.6 0.8 copy-done.2
  103.3 37.8 %newton_rows.1 = f32[8,128]{1,0:T(8,128)} custom-call(s32[4]{0:T(128)} %pad_add_fusion.where_ref, s32[8]{0:T(128)} %picks_ref.3, f32[8,72,128]{2,1,0:T(8,128)} %copy-done, f32[768,128]{1,0:T(8,128)} %copy-done.1, f32[768,128]{1,0:T(8,128)} %copy-done.2), custom_call_target="tpu_custom_call" | custom-call | tf_op jit(solution)/shard_map/newton_rows/pallas_call | solution.py:230
  141.2 0.7 broadcast_in_dim.16
  141.8 9.2 %all_to_all.22 = f32[16,8,128]{2,1,0:T(8,128)S(1)} all-to-all(f32[16,8,128]{2,1,0:T(8,128)S(1)} %broadcast_in_dim.16), channel_id=1, replica_groups=mesh['field_0'=4,'field_1'=4,'dom_0'=4,'dom_1'=2] {'field_0','field_1'}, dimensions={0} | all-to-all | bytes 131072 | tf_op jit(solution)/shard_map/all_to_all | solution.py:243
  151.1 0.6 copy.9
  (6 shorter events, 0.1 us)
Async XLA Ops:
  2.4 12.8 %all-to-all-start = ((f32[8,72,128]{2,1,0:T(8,128)}), f32[8,72,128]{2,1,0:T(8,128)S(1)}, u32[]{:S(2)}, u32[]{:S(2)}) async-start(f32[8,72,128]{2,1,0:T(8,128)} %broadcast_in_dim.14), calls=%async_computation | async-start | bytes 589824 | tf_op jit(solution)/shard_map/all_to_all | solution.py:243
  15.2 0.7 copy-start
  57.6 2.6 %collective-permute-start = (f32[768,128]{1,0:T(8,128)}, f32[768,128]{1,0:T(8,128)S(1)}, u32[]{:S(2)}, u32[]{:S(2)}) collective-permute-start(f32[768,128]{1,0:T(8,128)} %get-tuple-element.8), channel_id=1, source_target_pairs={{0,1},{1,0},{2,3},{3,2},{4,5},{5,4},{6,7},{7,6},{8,9},{9,8},{10,11... | collective-permute-start | bytes 1179656 | tf_op jit(solution)/shard_map/ppermute | solution.py:253
  97.9 4.7 %copy-start.1 = (f32[768,128]{1,0:T(8,128)}, f32[768,128]{1,0:T(8,128)S(1)}, u32[]{:S(2)}) copy-start(f32[768,128]{1,0:T(8,128)S(1)} %reshape.49.mine_ref) | copy-start | bytes 1179652
  97.9 4.7 %collective-permute-start.1 = (f32[768,128]{1,0:T(8,128)S(1)}, f32[768,128]{1,0:T(8,128)S(1)}, u32[]{:S(2)}, u32[]{:S(2)}) collective-permute-start(f32[768,128]{1,0:T(8,128)S(1)} %reshape.49.mine_ref), channel_id=1, source_target_pairs={{0,1},{1,0},{2,3},{3,2},{4,5},{5,4},{6,7},{7,6},{8,9},{9,8},{10,11... | collective-permute-start | bytes 1179656 | tf_op jit(solution)/shard_map/ppermute | solution.py:257
  102.6 0.8 copy-start.2

commit v2 on v1

--- a/solution.py
+++ b/solution.py
@@ -102,14 +102,114 @@
     )(snapshots, core, gathered, observed.reshape(1, count), precision.reshape(1, count), basis)
 
 
-def lane_of(rows, k):
-    return jnp.take_along_axis(rows, jnp.full(rows.shape, k, jnp.int32), axis=1)
+def tile_at(n):
+    return pl.ds(pl.multiple_of(n * 8, 8), 8)
+
+
+def factor_and_solve(sys_ref, panel_ref, wide_ref, rhs_ref, out_ref):
+    tiles = R // 8
+    sub = lax.broadcasted_iota(jnp.int32, (8, R), 0)
+
+    def row_of(ref, k, row):
+        return jnp.broadcast_to(ref[k, pl.ds(row, 1), :], (8, R))
+
+    def in_one_tile(rows):
+        out = rows[0]
+        for k in range(1, 8):
+            out = jnp.where(sub == k, rows[k], out)
+        return out
+
+    def panel(p, carry):
+        first = p * 8
+        corner = [[row_of(sys_ref, first + k, first + i) if i >= k else None for k in range(8)] for i in range(8)]
+        low = [[None] * 8 for _ in range(8)]
+        inverse = [None] * 8
+        for k in range(8):
+            inverse[k] = 1.0 / corner[k][k]
+            for i in range(k + 1, 8):
+                low[i][k] = corner[i][k] * inverse[k]
+            for j in range(k + 1, 8):
+                for i in range(j, 8):
+                    corner[i][j] = corner[i][j] - corner[i][k] * low[j][k]
+        y = [jnp.broadcast_to(rhs_ref[pl.ds(first + k, 1), :], (8, R)) for k in range(8)]
+        for k in range(8):
+            for m in range(k):
+                y[k] = y[k] - low[k][m] * y[m]
+        out_ref[tile_at(p), :] = in_one_tile([y[k] * inverse[k] for k in range(8)])
+
+        def below(t, carry):
+            at = tile_at(t)
+            columns = [sys_ref[first + k, at, :] for k in range(8)]
+            rhs = rhs_ref[at, :]
+            for k in range(8):
+                for m in range(k):
+                    columns[k] = columns[k] - columns[m] * low[k][m]
+                panel_ref[k, at, :] = columns[k]
+                factor = columns[k] * inverse[k]
+                sys_ref[first + k, at, :] = factor
+                for r in range(8):
+                    wide_ref[t * 8 + r, k] = jnp.broadcast_to(factor[r : r + 1], (8, R))
+                rhs = rhs - factor * y[k]
+            rhs_ref[at, :] = rhs
+            return carry
+
+        lax.fori_loop(p, tiles, below, 0)
+
+        def trailing(tj, carry):
+            def pair(h, carry):
+                at = [tile_at(tj + 2 * h), tile_at(tj + 2 * h + 1)]
+                columns = [[panel_ref[k, at[e], :] for k in range(8)] for e in range(2)]
+                for j in range(8):
+                    row = tj * 8 + j
+                    total = [None, None]
+                    for k in range(8):
+                        factor = wide_ref[row, k]
+                        for e in range(2):
+                            term = columns[e][k] * factor
+                            total[e] = term if k == 0 else total[e] + term
+                    for e in range(2):
+                        sys_ref[row, at[e], :] = sys_ref[row, at[e], :] - total[e]
+                return carry
+
+            return lax.fori_loop(0, (tiles - tj + 1) // 2, pair, carry)
+
+        return lax.fori_loop(p + 1, tiles, trailing, carry)
+
+    lax.fori_loop(0, tiles, panel, 0)
+
+    def back(n, carry):
+        p = tiles - 1 - n
+        first = p * 8
+
+        def gather(t, sums):
+            at = tile_at(t)
+            x = out_ref[at, :]
+            return tuple(sums[k] + sys_ref[first + k, at, :] * x for k in range(8))
+
+        sums = lax.fori_loop(p + 1, tiles, gather, tuple(jnp.zeros((8, R), f32) for _ in range(8)))
+        x = [
+            jnp.broadcast_to(out_ref[pl.ds(first + k, 1), :] - jnp.sum(sums[k], axis=0, keepdims=True), (8, R))
+            for k in range(8)
+        ]
+        for k in range(7, 0, -1):
+            for m in range(k):
+                x[m] = x[m] - row_of(sys_ref, first + m, first + k) * x[k]
+        out_ref[tile_at(p), :] = in_one_tile(x)
+        return carry
+
+    lax.fori_loop(0, tiles, back, 0)
+
+
+def in_three(x):
+    high = x.astype(bf16).astype(f32)
+    middle = (x - high).astype(bf16).astype(f32)
+    return high, middle, x - high - middle
 
 
 def steps_kernel(where_ref, picks_ref, gathered_ref, mine_ref, other_ref, out_ref,
-                 sums_ref, sys_ref):
+                 sums_ref, sys_ref, panel_ref, wide_ref, rhs_ref, step_ref):
     scale = R / PTS
-    core, dom, source, first = where_ref[0], where_ref[1], where_ref[2], where_ref[3]
+    core, dom = where_ref[0], where_ref[1]
     for half in range(2):
 
         @pl.when(core == half)
@@ -125,19 +225,22 @@
 
     everyone = particles(gathered_ref)
     tags = [gathered_ref[d, NP_DEV : NP_DEV + 1, :] for d in range(N_DOM)]
-    low = lane[0:1] < NP_DEV
+    first_half = lane[0:1] < NP_DEV
     counts = jnp.concatenate(
-        [jnp.where(low, tags[d], pltpu.roll(tags[d + 1], NP_DEV, 1)) for d in range(0, N_DOM, 2)], axis=1
+        [jnp.where(first_half, tags[d], pltpu.roll(tags[d + 1], NP_DEV, 1)) for d in range(0, N_DOM, 2)], axis=1
     )
 
-    owners = pltpu.roll(jnp.broadcast_to(gathered_ref[source, NP_DEV : NP_DEV + 1, :], (8, R)), NP_DEV, 1)
+    owners = pltpu.roll(jnp.concatenate(tags, axis=0), NP_DEV, 1)
     named = jnp.where((owners == dom.astype(f32)) & (lane < NP_DEV), 1.0, 0.0)
     before = jnp.dot(named, (square_r < square_q).astype(f32), precision=highest, preferred_element_type=f32)
-    slot = (sub + first).astype(f32)
-    choose = jnp.where((named > 0.5) & (before == slot), 1.0, 0.0)
-    valid = jnp.sum(choose, axis=1, keepdims=True)
-    own = jnp.dot(choose[:, :NP_DEV], gathered_ref[source, 0:NP_DEV, :], precision=highest,
-                  preferred_element_type=f32)
+    slot = lax.broadcasted_iota(jnp.int32, (16, R), 0).astype(f32)
+    own, valid = [], []
+    for d in range(N_DOM):
+        choose = jnp.where((named[d : d + 1] > 0.5) & (before[d : d + 1] == slot), 1.0, 0.0)
+        valid.append(jnp.sum(choose, axis=1, keepdims=True))
+        own.append(jnp.dot(choose[:, :NP_DEV], gathered_ref[d, 0:NP_DEV, :], precision=highest,
+                           preferred_element_type=f32))
+    own, valid = jnp.concatenate(own, axis=0), jnp.concatenate(valid, axis=0)
 
     mean_hess = sums_ref[NPART : NPART + R, :]
     for s in range(1, SNAP):
@@ -148,7 +251,7 @@
 
     lifted = jnp.dot(everyone, mean_hess, precision=highest, preferred_element_type=f32)
     ones = jnp.ones((8, R), f32)
-    norms = lax.dot_general(ones, lifted * everyone, last_pair, precision=highest, preferred_element_type=f32)
+    norms = lax.dot_general(ones, lifted * everyone, last_pair, precision=highest, preferred_element_type=f32)[0:1]
     own_lift = jnp.dot(own, mean_hess, precision=highest, preferred_element_type=f32)
     own_norm = jnp.sum(own_lift * own, axis=1, keepdims=True)
     cross = lax.dot_general(own_lift, everyone, last_pair, precision=highest, preferred_element_type=f32)
@@ -160,6 +263,7 @@
     numerator = jnp.dot(low_weights, carried, preferred_element_type=f32)
     grad = jnp.dot(low_weights.astype(f32), sums_ref[0:NPART, :], precision=highest, preferred_element_type=f32)
     drift = -(numerator + scale * grad) / total + repulse * own_lift
+    rhs_ref[...] = drift.T
 
     rows = []
     for s in range(SNAP):
@@ -169,59 +273,34 @@
     picked = jnp.concatenate(rows, axis=0)
     picked_lift = jnp.dot(picked, mean_hess, precision=highest, preferred_element_type=f32)
     picked_norm = lax.dot_general(ones, picked_lift * picked, last_pair, precision=highest,
-                                  preferred_element_type=f32)
+                                  preferred_element_type=f32)[0:1]
     picked_cross = lax.dot_general(own_lift, picked, last_pair, precision=highest, preferred_element_type=f32)
     apart = 1.0 + (own_norm + picked_norm - 2.0 * picked_cross) / trace
-    mixture = jnp.where(lane < SNAP, 1.0 / (apart * apart), 0.0)
+    mixture = jnp.where(square_q < SNAP, 1.0 / (apart * apart), 0.0)
     mixture = mixture / jnp.sum(mixture, axis=1, keepdims=True)
-
-    shares = [jnp.broadcast_to(mixture[:, s : s + 1], (8, R)) for s in range(SNAP)]
-    share_sum = functools.reduce(jnp.add, shares)
-    shares = [share * scale for share in shares]
+    shares = mixture.T[0:SNAP, :]
+    share_sum = jnp.sum(shares, axis=0, keepdims=True)
+    high, middle, low = in_three(shares * scale)
+    factors = jnp.concatenate([high, middle, low, high, middle, high], axis=0).astype(bf16)
 
     def assemble(g, carry):
-        tiles = [sums_ref[pl.ds(pl.multiple_of(NPART + s * R + g * 8, 8), 8), :] for s in range(SNAP)]
+        parts = []
         for k in range(8):
-            row = jnp.where(lane == g * 8 + k, share_sum, 0.0)
-            for s in range(SNAP):
-                row = row + shares[s] * tiles[s][k : k + 1, :]
-            sys_ref[g * 8 + k] = row
+            hess_rows = sums_ref[pl.ds(NPART + g * 8 + k, SNAP, stride=R), :]
+            high, middle, low = in_three(hess_rows)
+            parts.append(jnp.concatenate([high, high, high, middle, middle, low], axis=0).astype(bf16))
+        product = lax.dot_general(jnp.concatenate(parts, axis=1), factors, (((0,), (0,)), ((), ())),
+                                  preferred_element_type=f32)
+        for k in range(8):
+            sys_ref[g * 8 + k, 0:R, :] = product[k * R : (k + 1) * R]
+            sys_ref[g * 8 + k, tile_at(g), :] += jnp.where(sub == k, share_sum, 0.0)
         return carry
 
     lax.fori_loop(0, R // 8, assemble, 0)
-
-    def eliminate(start, h, carry):
-        rhs, inverses = carry
-        k = start + 2 * h
-        r0 = sys_ref[k]
-        i0 = 1.0 / lane_of(r0, k)
-        s0 = jnp.where(lane > k, r0, 0.0) * i0
-        r1 = sys_ref[k + 1] - lane_of(r0, k + 1) * s0
-        sys_ref[k + 1] = r1
-        i1 = 1.0 / lane_of(r1, k + 1)
-        m0 = jnp.where(lane > k + 1, r0, 0.0)
-        m1 = jnp.where(lane > k + 1, r1, 0.0)
-        s1 = m1 * i1
-        rhs = rhs - lane_of(rhs, k) * s0
-        rhs = rhs - lane_of(rhs, k + 1) * s1
-        inverses = jnp.where(lane == k, i0, jnp.where(lane == k + 1, i1, inverses))
-        for i in range(start, R):
-            sys_ref[i] = sys_ref[i] - m0[:, i : i + 1] * s0 - m1[:, i : i + 1] * s1
-        return rhs, inverses
-
-    carry = (drift, jnp.zeros((8, R), f32))
-    segment = R // 4
-    for start in range(0, R, segment):
-        carry = lax.fori_loop(0, segment // 2, functools.partial(eliminate, start), carry)
-    rhs, inverses = carry
-
-    def substitute(n, rhs):
-        m = R - 1 - n
-        x = lane_of(rhs * inverses, m)
-        return rhs - jnp.where(lane < m, sys_ref[m], 0.0) * x
-
-    rhs = lax.fori_loop(0, R, substitute, rhs, unroll=8)
-    out_ref[...] = jnp.where(valid > 0.5, own + rhs * inverses, 0.0)
+    sys_ref[:, R : R + 8, :] = jnp.zeros((R, 8, R), f32)
+    panel_ref[:, R : R + 8, :] = jnp.zeros((8, 8, R), f32)
+    factor_and_solve(sys_ref, panel_ref, wide_ref, rhs_ref, step_ref)
+    out_ref[...] = jnp.where(valid > 0.5, own + step_ref[...].T, 0.0)
 
 
 def newton_rows(where, snapshots, gathered, mine, other):
@@ -229,10 +308,17 @@
     smem = pl.BlockSpec(memory_space=pltpu.SMEM)
     return pl.pallas_call(
         steps_kernel,
-        out_shape=jax.ShapeDtypeStruct((8, R), f32),
+        out_shape=jax.ShapeDtypeStruct((R, R), f32),
         in_specs=[smem, smem, vmem, vmem, vmem],
         out_specs=vmem,
-        scratch_shapes=[pltpu.VMEM((ROWS, R), f32), pltpu.VMEM((R, 8, R), f32)],
+        scratch_shapes=[
+            pltpu.VMEM((ROWS, R), f32),
+            pltpu.VMEM((R, R + 8, R), f32),
+            pltpu.VMEM((8, R + 8, R), f32),
+            pltpu.VMEM((R, 8, 8, R), f32),
+            pltpu.VMEM((R, R), f32),
+            pltpu.VMEM((R, R), f32),
+        ],
         compiler_params=pltpu.CompilerParams(vmem_limit_bytes=VMEM_LIMIT),
         name="newton_rows",
     )(where, snapshots, gathered, mine, other)
@@ -255,10 +341,9 @@
     blocks = lax.all_to_all(part.reshape(chips, HALF // chips, R), CHIPS, 0, 0, tiled=True)
     mine = sent_to_all(jnp.sum(blocks, axis=0), CHIPS).reshape(HALF, R)
     other = lax.ppermute(mine, C, swap)
-    seat = lax.axis_index(FIELD)
-    where = jnp.stack([core, lax.axis_index(DOM), seat // 2, seat % 2 * 8])
+    where = jnp.stack([core, lax.axis_index(DOM)])
     rows = newton_rows(where, snapshots, gathered, mine, other)
-    return sent_to_all(rows, FIELD).reshape(1, N_DOM, 16, R)
+    return rows.reshape(1, N_DOM, 2 * NP_DEV // N_DOM, R)
 
 
 def solution(mesh):

time: 153 us -> 138 us (0.902)
  blocking collectives: 45.7 us -> 36.4 us
  Pallas kernels: 79.5 us -> 76 us
    all_to_all x2 -> x1, blocking collectives: 24.8 us -> 15.5 us  [sent_to_all(): return lax.all_to_all(copies, axes, split_axis=0, concat_axis=0, tiled=True)]
    pallas_call x1, Pallas kernels: 37.8 us -> 34.3 us  [newton_rows(): pl.pallas_call(steps_kernel, out_shape=jax.ShapeDtypeStruct((R, R), f32),...]
where the time goes in v2:
time: 138 us
  Pallas kernels  76 us (55%)
  blocking collectives  36.4 us (26%)
  starting transfers between devices  10.4 us (8%)
  waiting for transfers between devices  9.07 us (7%)
  other arithmetic  3.35 us (2%)
  local copies, waits for them, and re-layouts  2.38 us (2%)
    pallas_call x1, Pallas kernels, points_pass(): pl.pallas_call(functools.partial(points_kernel, block, chunk), out_shape=...  41.7 us
    pallas_call x1, Pallas kernels, newton_rows(): pl.pallas_call(steps_kernel, out_shape=jax.ShapeDtypeStruct((R, R), f32),...  34.3 us
    all_to_all x1, blocking collectives, body(): lax.all_to_all(part.reshape(chips, HALF // chips, R), CHIPS, 0, 0, tiled=...  20.9 us
    all_to_all x1, blocking collectives, sent_to_all(): return lax.all_to_all(copies, axes, split_axis=0, concat_axis=0, tiled=True)  15.5 us
    all_to_all x1, waiting for transfers between devices, sent_to_all(): return lax.all_to_all(copies, axes, split_axis=0, concat_axis=0, tiled=True)  6.81 us
    all_to_all x1, starting transfers between devices, sent_to_all(): return lax.all_to_all(copies, axes, split_axis=0, concat_axis=0, tiled=True)  5.97 us
    ppermute x1, starting transfers between devices, body(): other = lax.ppermute(mine, C, swap)  3.32 us
  transfers between devices with their start and end apart: 3, of which 3 were waited for; matrix products, arithmetic and copies ran while one was open for 0% of the time, Pallas kernels for 0%

profile of v2, /device:TPU:1, one launch (start us, length us, event | category | flops | bytes accessed | tf_op | source)
XLA Modules:
  0.0 137.7 jit_solution(4437855857957510322)
XLA Ops:
  0.0 0.7 add_convert_fusion
  0.7 0.1 pad.2.clone
  0.8 0.8 maximum_maximum_fusion
  1.7 0.7 broadcast_in_dim.11
  2.4 6.0 %all-to-all-start = ((f32[8,72,128]{2,1,0:T(8,128)}), f32[8,72,128]{2,1,0:T(8,128)S(1)}, u32[]{:S(2)}, u32[]{:S(2)}) async-start(f32[8,72,128]{2,1,0:T(8,128)} %broadcast_in_dim.11), calls=%async_computation | async-start | bytes 589824 | tf_op jit(solution)/shard_map/all_to_all | solution.py:329
  8.4 6.8 %all-to-all-done.gathered_ref = f32[8,72,128]{2,1,0:T(8,128)S(1)} async-done(((f32[8,72,128]{2,1,0:T(8,128)}), f32[8,72,128]{2,1,0:T(8,128)S(1)}, u32[]{:S(2)}, u32[]{:S(2)}) %all-to-all-start) | async-done | bytes 294944 | tf_op jit(solution)/shard_map/all_to_all | solution.py:329
  15.2 0.0 copy-start
  15.2 0.7 copy-done
  15.9 41.7 %points_pass.1 = (f32[768,128]{1,0:T(8,128)}, f32[768,128]{1,0:T(8,128)}) custom-call(s32[8]{0:T(128)} %picks_ref.3, s32[1]{0:T(128)} %bitcast.core_ref, f32[8,72,128]{2,1,0:T(8,128)} %copy-done, f32[1,32768]{1,0:T(1,128)} %bitcast.7, f32[1,32768]{1,0:T(1,128)} %bitcast.8, bf16[32768,128]{1,0:T(8,128)(2,1)} %basis_ref.1), custom_call_target="tpu_custom_call" | custom-call | tf_op jit(solution)/shard_map/points_pass/pallas_call | solution.py:80
  57.6 1.1 collective-permute-start
  58.7 1.6 %collective-permute-done = f32[768,128]{1,0:T(8,128)S(1)} collective-permute-done((f32[768,128]{1,0:T(8,128)}, f32[768,128]{1,0:T(8,128)S(1)}, u32[]{:S(2)}, u32[]{:S(2)}) %collective-permute-start) | collective-permute-done | bytes 393248 | tf_op jit(solution)/shard_map/ppermute | solution.py:339
  60.2 1.1 add.7
  61.3 20.9 %all_to_all.15 = f32[64,12,128]{2,1,0:T(8,128)S(1)} all-to-all(f32[64,12,128]{2,1,0:T(8,128)S(1)} %reshape.48), channel_id=1, replica_groups=mesh['field_0'=4,'field_1'=4,'dom_0'=4,'dom_1'=2] {'field_0','field_1','..., dimensions={0} | all-to-all | bytes 786432 | tf_op jit(solution)/shard_map/all_to_all | solution.py:341
  82.2 0.1 reduce_sum.9
  82.3 15.5 %all_to_all.16 = f32[64,12,128]{2,1,0:T(8,128)S(1)} all-to-all(f32[64,12,128]{2,1,0:T(8,128)S(1)} %broadcast_in_dim.12), channel_id=1, replica_groups=mesh['field_0'=4,'field_1'=4,'dom_0'=4,'dom_1'=2] {'field_0','field_1','..., dimensions={0} | all-to-all | bytes 786432 | tf_op jit(solution)/shard_map/all_to_all | solution.py:329
  97.9 0.0 copy-start.1
  97.9 3.3 %collective-permute-start.1 = (f32[768,128]{1,0:T(8,128)S(1)}, f32[768,128]{1,0:T(8,128)S(1)}, u32[]{:S(2)}, u32[]{:S(2)}) collective-permute-start(f32[768,128]{1,0:T(8,128)S(1)} %reshape.49.mine_ref), channel_id=1, source_target_pairs={{0,1},{1,0},{2,3},{3,2},{4,5},{5,4},{6,7},{7,6},{8,9},{9,8},{10,11... | collective-permute-start | bytes 1179656 | tf_op jit(solution)/shard_map/ppermute | solution.py:343
  101.2 0.6 pad_add_fusion.where_ref
  101.9 0.7 collective-permute-done.1.other_ref
  102.6 0.0 copy-done.1
  102.6 0.0 copy-start.2
  102.6 0.8 copy-done.2
  103.3 34.3 %newton_rows.1 = f32[128,128]{1,0:T(8,128)} custom-call(s32[2]{0:T(128)} %pad_add_fusion.where_ref, s32[8]{0:T(128)} %picks_ref.3, f32[8,72,128]{2,1,0:T(8,128)} %copy-done, f32[768,128]{1,0:T(8,128)} %copy-done.1, f32[768,128]{1,0:T(8,128)} %copy-done.2), custom_call_target="tpu_custom_call" | custom-call | tf_op jit(solution)/shard_map/newton_rows/pallas_call | solution.py:309
  (4 shorter events, 0.1 us)
Async XLA Ops:
  2.4 12.8 %all-to-all-start = ((f32[8,72,128]{2,1,0:T(8,128)}), f32[8,72,128]{2,1,0:T(8,128)S(1)}, u32[]{:S(2)}, u32[]{:S(2)}) async-start(f32[8,72,128]{2,1,0:T(8,128)} %broadcast_in_dim.11), calls=%async_computation | async-start | bytes 589824 | tf_op jit(solution)/shard_map/all_to_all | solution.py:329
  15.2 0.7 copy-start
  57.6 2.6 %collective-permute-start = (f32[768,128]{1,0:T(8,128)}, f32[768,128]{1,0:T(8,128)S(1)}, u32[]{:S(2)}, u32[]{:S(2)}) collective-permute-start(f32[768,128]{1,0:T(8,128)} %get-tuple-element.8), channel_id=1, source_target_pairs={{0,1},{1,0},{2,3},{3,2},{4,5},{5,4},{6,7},{7,6},{8,9},{9,8},{10,11... | collective-permute-start | bytes 1179656 | tf_op jit(solution)/shard_map/ppermute | solution.py:339
  97.9 4.7 %copy-start.1 = (f32[768,128]{1,0:T(8,128)}, f32[768,128]{1,0:T(8,128)S(1)}, u32[]{:S(2)}) copy-start(f32[768,128]{1,0:T(8,128)S(1)} %reshape.49.mine_ref) | copy-start | bytes 1179652
  97.9 4.7 %collective-permute-start.1 = (f32[768,128]{1,0:T(8,128)S(1)}, f32[768,128]{1,0:T(8,128)S(1)}, u32[]{:S(2)}, u32[]{:S(2)}) collective-permute-start(f32[768,128]{1,0:T(8,128)S(1)} %reshape.49.mine_ref), channel_id=1, source_target_pairs={{0,1},{1,0},{2,3},{3,2},{4,5},{5,4},{6,7},{7,6},{8,9},{9,8},{10,11... | collective-permute-start | bytes 1179656 | tf_op jit(solution)/shard_map/ppermute | solution.py:343
  102.6 0.8 copy-start.2

commit v3 on v2

--- a/solution.py
+++ b/solution.py
@@ -25,14 +25,36 @@
 f32, bf16 = jnp.float32, jnp.bfloat16
 highest = lax.Precision.HIGHEST
 last_pair = (((1,), (1,)), ((), ()))
-VMEM_LIMIT = 60 << 20
+POINTS_VMEM = 55 << 20
+STEPS_VMEM = 30 << 20
+
+
+def lines_kernel(coef_ref, copies_ref, owner_ref, lines_ref):
+    row = lax.broadcasted_iota(jnp.int32, (NP_DEV, R), 0)
+    lane = lax.broadcasted_iota(jnp.int32, (NP_DEV, R), 1)
+    owners = jnp.where(lane == row + NP_DEV, owner_ref[...], 0)
+    owners = jnp.sum(owners.astype(f32), axis=0, keepdims=True)
+    counts = jnp.concatenate([copies_ref[...].astype(f32), jnp.zeros((1, R - NP_DEV), f32)], axis=1)
+    for d in range(N_DOM):
+        lines_ref[d, 0:NP_DEV, :] = coef_ref[...]
+        lines_ref[d, NP_DEV : NP_DEV + 1, :] = owners + counts
+        lines_ref[d, NP_DEV + 1 : LINES, :] = jnp.zeros((LINES - NP_DEV - 1, R), f32)
+
+
+def packed_lines(coefficients, copies, owner):
+    return pl.pallas_call(
+        lines_kernel,
+        out_shape=jax.ShapeDtypeStruct((N_DOM, LINES, R), f32),
+        compiler_params=pltpu.CompilerParams(vmem_limit_bytes=4 << 20),
+        name="packed_lines",
+    )(coefficients, copies.reshape(1, NP_DEV), owner)
 
 
 def particles(gathered_ref):
     return jnp.concatenate([gathered_ref[d, 0:NP_DEV, :] for d in range(N_DOM)], axis=0)
 
 
-def points_kernel(block, chunk, picks_ref, core_ref, gathered_ref, obs_ref, prec_ref, basis_ref,
+def points_kernel(block, chunk, picks_ref, gathered_ref, obs_ref, prec_ref, basis_ref,
                   keep_ref, send_ref, coef_ref, sums_ref, left_ref, right_ref):
     step = pl.program_id(0)
 
@@ -67,21 +89,21 @@
     def _():
         for core in range(2):
 
-            @pl.when(core_ref[0] == core)
+            @pl.when(lax.axis_index(C) == core)
             def _():
                 keep_ref[...] = sums_ref[core * HALF : (core + 1) * HALF, :]
                 send_ref[...] = sums_ref[(1 - core) * HALF : (2 - core) * HALF, :]
 
 
-def points_pass(snapshots, core, gathered, observed, precision, basis):
-    block, chunk = 2048, 256
+def points_pass(snapshots, gathered, observed, precision, basis):
+    block, chunk = 4096, 512
     count = basis.shape[0]
     whole = lambda i, *_: (0, 0)
     return pl.pallas_call(
         functools.partial(points_kernel, block, chunk),
         out_shape=[jax.ShapeDtypeStruct((HALF, R), f32)] * 2,
         grid_spec=pltpu.PrefetchScalarGridSpec(
-            num_scalar_prefetch=2,
+            num_scalar_prefetch=1,
             grid=(count // block,),
             in_specs=[
                 pl.BlockSpec((N_DOM, LINES, R), lambda i, *_: (0, 0, 0)),
@@ -97,9 +119,9 @@
                 pltpu.VMEM((block, R), bf16),
             ],
         ),
-        compiler_params=pltpu.CompilerParams(vmem_limit_bytes=VMEM_LIMIT),
+        compiler_params=pltpu.CompilerParams(vmem_limit_bytes=POINTS_VMEM),
         name="points_pass",
-    )(snapshots, core, gathered, observed.reshape(1, count), precision.reshape(1, count), basis)
+    )(snapshots, gathered, observed.reshape(1, count), precision.reshape(1, count), basis)
 
 
 def tile_at(n):
@@ -156,22 +178,24 @@
         lax.fori_loop(p, tiles, below, 0)
 
         def trailing(tj, carry):
-            def pair(h, carry):
-                at = [tile_at(tj + 2 * h), tile_at(tj + 2 * h + 1)]
-                columns = [[panel_ref[k, at[e], :] for k in range(8)] for e in range(2)]
+            def group(size, start, h, carry):
+                at = [tile_at(start + size * h + e) for e in range(size)]
+                columns = [[panel_ref[k, at[e], :] for k in range(8)] for e in range(size)]
                 for j in range(8):
                     row = tj * 8 + j
-                    total = [None, None]
+                    total = [None] * size
                     for k in range(8):
                         factor = wide_ref[row, k]
-                        for e in range(2):
+                        for e in range(size):
                             term = columns[e][k] * factor
                             total[e] = term if k == 0 else total[e] + term
-                    for e in range(2):
+                    for e in range(size):
                         sys_ref[row, at[e], :] = sys_ref[row, at[e], :] - total[e]
                 return carry
 
-            return lax.fori_loop(0, (tiles - tj + 1) // 2, pair, carry)
+            rest = (tiles - tj) % 3
+            lax.fori_loop(0, rest, functools.partial(group, 1, tj), carry)
+            return lax.fori_loop(0, (tiles - tj) // 3, functools.partial(group, 3, tj + rest), carry)
 
         return lax.fori_loop(p + 1, tiles, trailing, carry)
 
@@ -206,10 +230,10 @@
     return high, middle, x - high - middle
 
 
-def steps_kernel(where_ref, picks_ref, gathered_ref, mine_ref, other_ref, out_ref,
+def steps_kernel(picks_ref, gathered_ref, mine_ref, other_ref, out_ref,
                  sums_ref, sys_ref, panel_ref, wide_ref, rhs_ref, step_ref):
     scale = R / PTS
-    core, dom = where_ref[0], where_ref[1]
+    core, dom = lax.axis_index(C), lax.axis_index(DOM)
     for half in range(2):
 
         @pl.when(core == half)
@@ -292,36 +316,34 @@
         product = lax.dot_general(jnp.concatenate(parts, axis=1), factors, (((0,), (0,)), ((), ())),
                                   preferred_element_type=f32)
         for k in range(8):
-            sys_ref[g * 8 + k, 0:R, :] = product[k * R : (k + 1) * R]
+            sys_ref[g * 8 + k] = product[k * R : (k + 1) * R]
             sys_ref[g * 8 + k, tile_at(g), :] += jnp.where(sub == k, share_sum, 0.0)
         return carry
 
-    lax.fori_loop(0, R // 8, assemble, 0)
-    sys_ref[:, R : R + 8, :] = jnp.zeros((R, 8, R), f32)
-    panel_ref[:, R : R + 8, :] = jnp.zeros((8, 8, R), f32)
+    lax.fori_loop(0, R // 8, assemble, 0, unroll=4)
     factor_and_solve(sys_ref, panel_ref, wide_ref, rhs_ref, step_ref)
     out_ref[...] = jnp.where(valid > 0.5, own + step_ref[...].T, 0.0)
 
 
-def newton_rows(where, snapshots, gathered, mine, other):
+def newton_rows(snapshots, gathered, mine, other):
     vmem = pl.BlockSpec(memory_space=pltpu.VMEM)
     smem = pl.BlockSpec(memory_space=pltpu.SMEM)
     return pl.pallas_call(
         steps_kernel,
         out_shape=jax.ShapeDtypeStruct((R, R), f32),
-        in_specs=[smem, smem, vmem, vmem, vmem],
+        in_specs=[smem, vmem, vmem, vmem],
         out_specs=vmem,
         scratch_shapes=[
             pltpu.VMEM((ROWS, R), f32),
-            pltpu.VMEM((R, R + 8, R), f32),
-            pltpu.VMEM((8, R + 8, R), f32),
+            pltpu.VMEM((R, R, R), f32),
+            pltpu.VMEM((8, R, R), f32),
             pltpu.VMEM((R, 8, 8, R), f32),
             pltpu.VMEM((R, R), f32),
             pltpu.VMEM((R, R), f32),
         ],
-        compiler_params=pltpu.CompilerParams(vmem_limit_bytes=VMEM_LIMIT),
+        compiler_params=pltpu.CompilerParams(vmem_limit_bytes=STEPS_VMEM),
         name="newton_rows",
-    )(where, snapshots, gathered, mine, other)
+    )(snapshots, gathered, mine, other)
 
 
 def sent_to_all(shard, axes):
@@ -330,19 +352,16 @@
 
 
 def body(coefficients, copies, owner, snapshots, basis, observed, precision):
-    tags = jnp.concatenate([copies, owner[:, 0]]).astype(f32)[None]
-    lines = jnp.concatenate([coefficients, tags, jnp.zeros((LINES - NP_DEV - 1, R), f32)], axis=0)
-    gathered = sent_to_all(lines, DOM)
-    core = lax.axis_index(C)
+    lines = packed_lines(coefficients, copies, owner)
+    gathered = lax.all_to_all(lines, DOM, split_axis=0, concat_axis=0, tiled=True)
     swap = [(0, 1), (1, 0)]
-    keep, send = points_pass(snapshots, core.reshape(1), gathered, observed, precision, basis)
+    keep, send = points_pass(snapshots, gathered, observed, precision, basis)
     part = keep + lax.ppermute(send, C, swap)
     chips = lax.axis_size(CHIPS)
     blocks = lax.all_to_all(part.reshape(chips, HALF // chips, R), CHIPS, 0, 0, tiled=True)
     mine = sent_to_all(jnp.sum(blocks, axis=0), CHIPS).reshape(HALF, R)
     other = lax.ppermute(mine, C, swap)
-    where = jnp.stack([core, lax.axis_index(DOM)])
-    rows = newton_rows(where, snapshots, gathered, mine, other)
+    rows = newton_rows(snapshots, gathered, mine, other)
     return rows.reshape(1, N_DOM, 2 * NP_DEV // N_DOM, R)
 
 

time: 138 us -> 131 us (0.949)
  blocking collectives: 36.4 us -> 49.6 us
  starting transfers between devices: 10.4 us -> 3.89 us
  waiting for transfers between devices: 9.07 us -> 2.91 us
  Pallas kernels: 76 us -> 71.1 us
  other arithmetic: 3.35 us -> 1.13 us
    all_to_all x0 -> x1, blocking collectives: none -> 13.2 us  [body(): lax.all_to_all(lines, DOM, split_axis=0, concat_axis=0, tiled=True)]
    all_to_all x1 -> x0, waiting for transfers between devices: 6.81 us -> none  [sent_to_all(): return lax.all_to_all(copies, axes, split_axis=0, concat_axis=0, tiled=True)]
    all_to_all x1 -> x0, starting transfers between devices: 5.97 us -> none  [sent_to_all(): return lax.all_to_all(copies, axes, split_axis=0, concat_axis=0, tiled=True)]
    pallas_call x1, Pallas kernels: 34.3 us -> 30.7 us  [newton_rows(): pl.pallas_call(steps_kernel, out_shape=jax.ShapeDtypeStruct((R, R), f32),...]
  transfers between devices with their start and end apart: 3 -> 2, of which waited for: 3 -> 2; matrix products, arithmetic and copies ran while one was open for 0% -> 0% of each run, Pallas kernels for 0% -> 0%
where the time goes in v3:
time: 131 us
  Pallas kernels  71.1 us (54%)
  blocking collectives  49.6 us (38%)
  starting transfers between devices  3.89 us (3%)
  waiting for transfers between devices  2.91 us (2%)
  local copies, waits for them, and re-layouts  2.29 us (2%)
    pallas_call x1, Pallas kernels, points_pass(): pl.pallas_call(functools.partial(points_kernel, block, chunk), out_shape=...  40.4 us
    pallas_call x1, Pallas kernels, newton_rows(): pl.pallas_call(steps_kernel, out_shape=jax.ShapeDtypeStruct((R, R), f32),...  30.7 us
    all_to_all x1, blocking collectives, body(): lax.all_to_all(part.reshape(chips, HALF // chips, R), CHIPS, 0, 0, tiled=...  20.9 us
    all_to_all x1, blocking collectives, sent_to_all(): return lax.all_to_all(copies, axes, split_axis=0, concat_axis=0, tiled=True)  15.5 us
    all_to_all x1, blocking collectives, body(): lax.all_to_all(lines, DOM, split_axis=0, concat_axis=0, tiled=True)  13.2 us
    ppermute x1, starting transfers between devices, body(): other = lax.ppermute(mine, C, swap)  3.32 us
  transfers between devices with their start and end apart: 2, of which 2 were waited for; matrix products, arithmetic and copies ran while one was open for 0% of the time, Pallas kernels for 0%

profile of v3, /device:TPU:1, one launch (start us, length us, event | category | flops | bytes accessed | tf_op | source)
XLA Modules:
  0.0 131.0 jit_solution(9516414094034083389)
XLA Ops:
  0.0 0.0 copy-start.2
  0.0 0.8 copy.9.owner_ref
  0.8 0.0 copy-start.1
  0.8 0.8 copy-done.1
  1.5 0.0 copy-start.3
  1.5 0.7 copy-done.3
  2.2 0.1 packed_lines.1
  2.3 13.2 %all_to_all.15.gathered_ref = f32[8,72,128]{2,1,0:T(8,128)} all-to-all(f32[8,72,128]{2,1,0:T(8,128)S(1)} %packed_lines.1), channel_id=1, replica_groups=mesh['field_0'=4,'field_1'=4,'dom_0'=4,'dom_1'=2] {'dom_0','dom_1'}, dimensions={0} | all-to-all | bytes 589824 | tf_op jit(solution)/shard_map/all_to_all | solution.py:356
  15.5 0.0 copy-start
  15.5 40.4 %points_pass.1 = (f32[768,128]{1,0:T(8,128)}, f32[768,128]{1,0:T(8,128)}) custom-call(s32[8]{0:T(128)} %picks_ref.3, f32[8,72,128]{2,1,0:T(8,128)} %all_to_all.15.gathered_ref, f32[1,32768]{1,0:T(1,128)} %bitcast.5, f32[1,32768]{1,0:T(1,128)} %bitcast.6, bf16[32768,128]{1,0:T(8,128)(2,1)} %basis_ref.1), custom_call_target="tpu_custom_call" | custom-call | tf_op jit(solution)/shard_map/points_pass/pallas_call | solution.py:102
  55.8 0.6 collective-permute-start
  56.4 1.6 %collective-permute-done = f32[768,128]{1,0:T(8,128)S(1)} collective-permute-done((f32[768,128]{1,0:T(8,128)}, f32[768,128]{1,0:T(8,128)S(1)}, u32[]{:S(2)}, u32[]{:S(2)}) %collective-permute-start) | collective-permute-done | bytes 393248 | tf_op jit(solution)/shard_map/ppermute | solution.py:359
  58.0 1.1 add.3
  59.1 20.9 %all_to_all.16 = f32[64,12,128]{2,1,0:T(8,128)S(1)} all-to-all(f32[64,12,128]{2,1,0:T(8,128)S(1)} %reshape.21), channel_id=1, replica_groups=mesh['field_0'=4,'field_1'=4,'dom_0'=4,'dom_1'=2] {'field_0','field_1','..., dimensions={0} | all-to-all | bytes 786432 | tf_op jit(solution)/shard_map/all_to_all | solution.py:361
  79.9 0.1 reduce_sum.9
  80.1 15.5 %all_to_all.17 = f32[64,12,128]{2,1,0:T(8,128)S(1)} all-to-all(f32[64,12,128]{2,1,0:T(8,128)S(1)} %broadcast_in_dim.3), channel_id=1, replica_groups=mesh['field_0'=4,'field_1'=4,'dom_0'=4,'dom_1'=2] {'field_0','field_1','..., dimensions={0} | all-to-all | bytes 786432 | tf_op jit(solution)/shard_map/all_to_all | solution.py:351
  95.6 3.3 %collective-permute-start.1 = (f32[768,128]{1,0:T(8,128)S(1)}, f32[768,128]{1,0:T(8,128)S(1)}, u32[]{:S(2)}, u32[]{:S(2)}) collective-permute-start(f32[768,128]{1,0:T(8,128)S(1)} %reshape.22.mine_ref), channel_id=1, source_target_pairs={{0,1},{1,0},{2,3},{3,2},{4,5},{5,4},{6,7},{7,6},{8,9},{9,8},{10,11... | collective-permute-start | bytes 1179656 | tf_op jit(solution)/shard_map/ppermute | solution.py:363
  99.0 1.3 %collective-permute-done.1.other_ref = f32[768,128]{1,0:T(8,128)S(1)} collective-permute-done((f32[768,128]{1,0:T(8,128)S(1)}, f32[768,128]{1,0:T(8,128)S(1)}, u32[]{:S(2)}, u32[]{:S(2)}) %collective-permute-start.1) | collective-permute-done | bytes 393248 | tf_op jit(solution)/shard_map/ppermute | solution.py:363
  100.3 0.0 copy-done.2
  100.3 0.0 copy-done
  100.3 30.7 %newton_rows.1 = f32[128,128]{1,0:T(8,128)} custom-call(s32[8]{0:T(128)S(1)} %copy-done.2, f32[8,72,128]{2,1,0:T(8,128)S(1)} %copy-done, f32[768,128]{1,0:T(8,128)S(1)} %reshape.22.mine_ref, f32[768,128]{1,0:T(8,128)S(1)} %collective-permute-done.1.other_ref), custom_call_target="tpu_custom_call" | custom-call | tf_op jit(solution)/shard_map/newton_rows/pallas_call | solution.py:331
  (3 shorter events, 0.1 us)
Async XLA Ops:
  0.0 100.3 %copy-start.2 = (s32[8]{0:T(128)S(1)}, s32[8]{0:T(128)}, u32[]{:S(2)}) copy-start(s32[8]{0:T(128)} %picks_ref.3) | copy-start | bytes 100
  0.8 0.8 copy-start.1
  1.5 0.7 copy-start.3
  15.5 84.9 %copy-start = (f32[8,72,128]{2,1,0:T(8,128)S(1)}, f32[8,72,128]{2,1,0:T(8,128)}, u32[]{:S(2)}) copy-start(f32[8,72,128]{2,1,0:T(8,128)} %all_to_all.15.gathered_ref) | copy-start | bytes 884740
  55.8 2.1 %collective-permute-start = (f32[768,128]{1,0:T(8,128)}, f32[768,128]{1,0:T(8,128)S(1)}, u32[]{:S(2)}, u32[]{:S(2)}) collective-permute-start(f32[768,128]{1,0:T(8,128)} %get-tuple-element.8), channel_id=1, source_target_pairs={{0,1},{1,0},{2,3},{3,2},{4,5},{5,4},{6,7},{7,6},{8,9},{9,8},{10,11... | collective-permute-start | bytes 1179656 | tf_op jit(solution)/shard_map/ppermute | solution.py:359
  95.6 4.7 %collective-permute-start.1 = (f32[768,128]{1,0:T(8,128)S(1)}, f32[768,128]{1,0:T(8,128)S(1)}, u32[]{:S(2)}, u32[]{:S(2)}) collective-permute-start(f32[768,128]{1,0:T(8,128)S(1)} %reshape.22.mine_ref), channel_id=1, source_target_pairs={{0,1},{1,0},{2,3},{3,2},{4,5},{5,4},{6,7},{7,6},{8,9},{9,8},{10,11... | collective-permute-start | bytes 1179656 | tf_op jit(solution)/shard_map/ppermute | solution.py:363

commit v4 on v3

--- a/solution.py
+++ b/solution.py
@@ -25,42 +25,41 @@
 f32, bf16 = jnp.float32, jnp.bfloat16
 highest = lax.Precision.HIGHEST
 last_pair = (((1,), (1,)), ((), ()))
-POINTS_VMEM = 55 << 20
+POINTS_VMEM = 51 << 20
 STEPS_VMEM = 30 << 20
 
 
 def lines_kernel(coef_ref, copies_ref, owner_ref, lines_ref):
-    row = lax.broadcasted_iota(jnp.int32, (NP_DEV, R), 0)
-    lane = lax.broadcasted_iota(jnp.int32, (NP_DEV, R), 1)
-    owners = jnp.where(lane == row + NP_DEV, owner_ref[...], 0)
-    owners = jnp.sum(owners.astype(f32), axis=0, keepdims=True)
-    counts = jnp.concatenate([copies_ref[...].astype(f32), jnp.zeros((1, R - NP_DEV), f32)], axis=1)
-    for d in range(N_DOM):
-        lines_ref[d, 0:NP_DEV, :] = coef_ref[...]
-        lines_ref[d, NP_DEV : NP_DEV + 1, :] = owners + counts
-        lines_ref[d, NP_DEV + 1 : LINES, :] = jnp.zeros((LINES - NP_DEV - 1, R), f32)
+    lines_ref[0:NP_DEV, :] = coef_ref[...]
+    tags = jnp.concatenate([copies_ref[...], owner_ref[...]], axis=1).astype(f32)
+    lines_ref[NP_DEV:LINES, :] = jnp.broadcast_to(tags, (LINES - NP_DEV, R))
 
 
 def packed_lines(coefficients, copies, owner):
     return pl.pallas_call(
         lines_kernel,
-        out_shape=jax.ShapeDtypeStruct((N_DOM, LINES, R), f32),
-        compiler_params=pltpu.CompilerParams(vmem_limit_bytes=4 << 20),
+        out_shape=jax.ShapeDtypeStruct((LINES, R), f32),
+        compiler_params=pltpu.CompilerParams(vmem_limit_bytes=60 << 20),
         name="packed_lines",
-    )(coefficients, copies.reshape(1, NP_DEV), owner)
+    )(coefficients, copies.reshape(1, NP_DEV), owner.reshape(1, NP_DEV))
 
 
 def particles(gathered_ref):
     return jnp.concatenate([gathered_ref[d, 0:NP_DEV, :] for d in range(N_DOM)], axis=0)
 
 
-def points_kernel(block, chunk, picks_ref, gathered_ref, obs_ref, prec_ref, basis_ref,
-                  keep_ref, send_ref, coef_ref, sums_ref, left_ref, right_ref):
+def points_kernel(block, chunk, picks_ref, near_ref, one_ref, two_ref, three_ref, obs_ref, prec_ref, basis_ref,
+                  gathered_ref, keep_ref, send_ref, coef_ref, sums_ref, left_ref, right_ref):
     step = pl.program_id(0)
 
     @pl.when(step == 0)
     def _():
         sums_ref[...] = jnp.zeros_like(sums_ref)
+        y, core = lax.axis_index(Y), lax.axis_index(C)
+        for shift, pair_ref in enumerate((near_ref, one_ref, two_ref, three_ref)):
+            for j in range(2):
+                source = (y + 4 - shift) % 4 * 2 + (core + j) % 2
+                gathered_ref[source] = pair_ref[j * LINES : (j + 1) * LINES, :]
         coef_ref[0:NPART, :] = particles(gathered_ref).astype(bf16)
         rows = []
         for s in range(SNAP):
@@ -95,23 +94,27 @@
                 send_ref[...] = sums_ref[(1 - core) * HALF : (2 - core) * HALF, :]
 
 
-def points_pass(snapshots, gathered, observed, precision, basis):
+def in_hbm(x):
+    return pltpu.with_memory_space_constraint(x, pltpu.HBM)
+
+
+def points_pass(snapshots, pairs, observed, precision, basis):
     block, chunk = 4096, 512
     count = basis.shape[0]
     whole = lambda i, *_: (0, 0)
     return pl.pallas_call(
         functools.partial(points_kernel, block, chunk),
-        out_shape=[jax.ShapeDtypeStruct((HALF, R), f32)] * 2,
+        out_shape=[jax.ShapeDtypeStruct((N_DOM, LINES, R), f32)] + [jax.ShapeDtypeStruct((HALF, R), f32)] * 2,
         grid_spec=pltpu.PrefetchScalarGridSpec(
             num_scalar_prefetch=1,
             grid=(count // block,),
             in_specs=[
-                pl.BlockSpec((N_DOM, LINES, R), lambda i, *_: (0, 0, 0)),
+                *[pl.BlockSpec((2 * LINES, R), whole)] * 4,
                 pl.BlockSpec((1, block), lambda i, *_: (0, i)),
                 pl.BlockSpec((1, block), lambda i, *_: (0, i)),
                 pl.BlockSpec((block, R), lambda i, *_: (i, 0)),
             ],
-            out_specs=[pl.BlockSpec((HALF, R), whole)] * 2,
+            out_specs=[pl.BlockSpec((N_DOM, LINES, R), lambda i, *_: (0, 0, 0))] + [pl.BlockSpec((HALF, R), whole)] * 2,
             scratch_shapes=[
                 pltpu.VMEM((NPART + 16, R), bf16),
                 pltpu.VMEM((ROWS, R), f32),
@@ -121,7 +124,7 @@
         ),
         compiler_params=pltpu.CompilerParams(vmem_limit_bytes=POINTS_VMEM),
         name="points_pass",
-    )(snapshots, gathered, observed.reshape(1, count), precision.reshape(1, count), basis)
+    )(in_hbm(snapshots), *pairs, *[in_hbm(a.reshape(1, count)) for a in (observed, precision)], basis)
 
 
 def tile_at(n):
@@ -352,10 +355,11 @@
 
 
 def body(coefficients, copies, owner, snapshots, basis, observed, precision):
+    swap = [(0, 1), (1, 0)]
     lines = packed_lines(coefficients, copies, owner)
-    gathered = lax.all_to_all(lines, DOM, split_axis=0, concat_axis=0, tiled=True)
-    swap = [(0, 1), (1, 0)]
-    keep, send = points_pass(snapshots, gathered, observed, precision, basis)
+    pair = jnp.concatenate([lines, lax.ppermute(lines, C, swap)], axis=0)
+    pairs = [pair] + [lax.ppermute(pair, Y, [(y, (y + shift) % 4) for y in range(4)]) for shift in (1, 2, 3)]
+    gathered, keep, send = points_pass(snapshots, pairs, observed, precision, basis)
     part = keep + lax.ppermute(send, C, swap)
     chips = lax.axis_size(CHIPS)
     blocks = lax.all_to_all(part.reshape(chips, HALF // chips, R), CHIPS, 0, 0, tiled=True)

time: 131 us -> 128 us (0.977)
  blocking collectives: 49.6 us -> 36.2 us
  waiting for transfers between devices: 2.91 us -> 9.58 us
  starting transfers between devices: 3.89 us -> 9.6 us
  local copies, waits for them, and re-layouts: 2.29 us -> 0.11 us
    all_to_all x1 -> x0, blocking collectives: 13.2 us -> none  [body(): lax.all_to_all(lines, DOM, split_axis=0, concat_axis=0, tiled=True)]
    ppermute x0 -> x4, waiting for transfers between devices: none -> 6.88 us  [the longest x3 5.81 us: body(): lax.ppermute(pair, Y, [(y, (y + shift) % 4) for y in range(4)])]
    ppermute x0 -> x4, starting transfers between devices: none -> 5.28 us  [the longest x3 3.86 us: body(): lax.ppermute(pair, Y, [(y, (y + shift) % 4) for y in range(4)])]
    unnamed x9 -> x2, local copies, waits for them, and re-layouts: 2.18 us -> 0.01 us
    pallas_call x1, Pallas kernels: 0.09 us -> 1.47 us  [packed_lines(): pl.pallas_call(lines_kernel, out_shape=jax.ShapeDtypeStruct((LINES, R), f...]
  transfers between devices with their start and end apart: 2 -> 6, of which waited for: 2 -> 6; matrix products, arithmetic and copies ran while one was open for 0% -> 0% of each run, Pallas kernels for 0% -> 0%
where the time goes in v4:
time: 128 us
  Pallas kernels  71.6 us (56%)
  blocking collectives  36.2 us (28%)
  starting transfers between devices  9.6 us (8%)
  waiting for transfers between devices  9.58 us (7%)
    pallas_call x1, Pallas kernels, points_pass(): pl.pallas_call(functools.partial(points_kernel, block, chunk), out_shape=...  39.3 us
    pallas_call x1, Pallas kernels, newton_rows(): pl.pallas_call(steps_kernel, out_shape=jax.ShapeDtypeStruct((R, R), f32),...  30.8 us
    all_to_all x1, blocking collectives, body(): lax.all_to_all(part.reshape(chips, HALF // chips, R), CHIPS, 0, 0, tiled=...  20.7 us
    all_to_all x1, blocking collectives, sent_to_all(): return lax.all_to_all(copies, axes, split_axis=0, concat_axis=0, tiled=True)  15.5 us
    ppermute x3, waiting for transfers between devices, body(): lax.ppermute(pair, Y, [(y, (y + shift) % 4) for y in range(4)])  5.81 us
    ppermute x3, starting transfers between devices, body(): lax.ppermute(pair, Y, [(y, (y + shift) % 4) for y in range(4)])  3.86 us
    ppermute x1, starting transfers between devices, body(): other = lax.ppermute(mine, C, swap)  3.32 us
  transfers between devices with their start and end apart: 6, of which 6 were waited for; matrix products, arithmetic and copies ran while one was open for 0% of the time, Pallas kernels for 0%

profile of v4, /device:TPU:1, one launch (start us, length us, event | category | flops | bytes accessed | tf_op | source)
XLA Modules:
  0.0 128.0 jit_solution(3468774790111025048)
XLA Ops:
  0.0 0.0 copy-start
  0.0 1.5 %packed_lines.1 = f32[72,128]{1,0:T(8,128)} custom-call(f32[64,128]{1,0:T(8,128)} %coef_ref.1, s32[1,64]{1,0:T(1,128)} %bitcast.7, s32[1,64]{1,0:T(1,128)} %bitcast.8), custom_call_target="tpu_custom_call" | custom-call | tf_op jit(solution)/shard_map/packed_lines/pallas_call | solution.py:39
  1.5 1.4 %collective-permute-start = (f32[72,128]{1,0:T(8,128)}, f32[72,128]{1,0:T(8,128)S(1)}, u32[]{:S(2)}, u32[]{:S(2)}) collective-permute-start(f32[72,128]{1,0:T(8,128)} %packed_lines.1), channel_id=1, source_target_pairs={{0,1},{1,0},{2,3},{3,2},{4,5},{5,4},{6,7},{7,6},{8,9},{9,8},{10,11... | collective-permute-start | bytes 110600 | tf_op jit(solution)/shard_map/ppermute | solution.py:360
  2.9 1.1 collective-permute-done
  4.0 0.8 pad_maximum_fusion.near_ref
  4.7 2.8 %collective-permute-start.3 = (f32[144,128]{1,0:T(8,128)S(1)}, f32[144,128]{1,0:T(8,128)S(1)}, u32[]{:S(2)}, u32[]{:S(2)}) collective-permute-start(f32[144,128]{1,0:T(8,128)S(1)} %pad_maximum_fusion.near_ref), channel_id=1, source_target_pairs={{0,6},{2,0},{4,2},{6,4},{1,7},{3,1},{5,3},{7,5},{8,14},{10,8},{12,... | collective-permute-start | bytes 221192 | tf_op jit(solution)/shard_map/ppermute | solution.py:361
  7.6 0.3 collective-permute-start.2
  7.9 0.7 collective-permute-start.1
  8.6 0.4 collective-permute-done.3.three_ref
  9.0 3.4 %collective-permute-done.2.two_ref = f32[144,128]{1,0:T(8,128)S(1)} collective-permute-done((f32[144,128]{1,0:T(8,128)S(1)}, f32[144,128]{1,0:T(8,128)S(1)}, u32[]{:S(2)}, u32[]{:S(2)}) %collective-permute-start.2) | collective-permute-done | bytes 73760 | tf_op jit(solution)/shard_map/ppermute | solution.py:361
  12.4 2.1 %collective-permute-done.1.one_ref = f32[144,128]{1,0:T(8,128)S(1)} collective-permute-done((f32[144,128]{1,0:T(8,128)S(1)}, f32[144,128]{1,0:T(8,128)S(1)}, u32[]{:S(2)}, u32[]{:S(2)}) %collective-permute-start.1) | collective-permute-done | bytes 73760 | tf_op jit(solution)/shard_map/ppermute | solution.py:361
  14.4 39.3 %points_pass.1 = (f32[8,72,128]{2,1,0:T(8,128)S(1)}, f32[768,128]{1,0:T(8,128)S(1)}, f32[768,128]{1,0:T(8,128)S(1)}) custom-call(s32[8]{0:T(128)} %picks_ref.3, f32[144,128]{1,0:T(8,128)S(1)} %pad_maximum_fusion.near_ref, f32[144,128]{1,0:T(8,128)S(1)} %collective-permute-done.1.one_ref, f32[144,128]{1,0:T(8,128)S(1)} %collective-permute-done.2.two_ref, ...), custom_call_target="tpu_custom_call" | custom-call | tf_op jit(solution)/shard_map/points_pass/pallas_call | solution.py:105
  53.7 1.0 collective-permute-start.4
  54.7 1.3 %collective-permute-done.4 = f32[768,128]{1,0:T(8,128)S(1)} collective-permute-done((f32[768,128]{1,0:T(8,128)S(1)}, f32[768,128]{1,0:T(8,128)S(1)}, u32[]{:S(2)}, u32[]{:S(2)}) %collective-permute-start.4) | collective-permute-done | bytes 393248 | tf_op jit(solution)/shard_map/ppermute | solution.py:363
  56.2 20.7 %all_to_all.10 = f32[64,12,128]{2,1,0:T(8,128)S(1)} all-to-all(f32[64,12,128]{2,1,0:T(8,128)S(1)} %reshape.25), channel_id=1, replica_groups=mesh['field_0'=4,'field_1'=4,'dom_0'=4,'dom_1'=2] {'field_0','field_1','..., dimensions={0} | all-to-all | bytes 786432 | tf_op jit(solution)/shard_map/all_to_all | solution.py:365
  76.8 0.1 reduce_sum.9
  77.0 15.5 %all_to_all.11 = f32[64,12,128]{2,1,0:T(8,128)S(1)} all-to-all(f32[64,12,128]{2,1,0:T(8,128)S(1)} %broadcast_in_dim.3), channel_id=1, replica_groups=mesh['field_0'=4,'field_1'=4,'dom_0'=4,'dom_1'=2] {'field_0','field_1','..., dimensions={0} | all-to-all | bytes 786432 | tf_op jit(solution)/shard_map/all_to_all | solution.py:354
  92.6 3.3 %collective-permute-start.5 = (f32[768,128]{1,0:T(8,128)S(1)}, f32[768,128]{1,0:T(8,128)S(1)}, u32[]{:S(2)}, u32[]{:S(2)}) collective-permute-start(f32[768,128]{1,0:T(8,128)S(1)} %reshape.26.mine_ref), channel_id=1, source_target_pairs={{0,1},{1,0},{2,3},{3,2},{4,5},{5,4},{6,7},{7,6},{8,9},{9,8},{10,11... | collective-permute-start | bytes 1179656 | tf_op jit(solution)/shard_map/ppermute | solution.py:367
  95.9 1.3 %collective-permute-done.5.other_ref = f32[768,128]{1,0:T(8,128)S(1)} collective-permute-done((f32[768,128]{1,0:T(8,128)S(1)}, f32[768,128]{1,0:T(8,128)S(1)}, u32[]{:S(2)}, u32[]{:S(2)}) %collective-permute-start.5) | collective-permute-done | bytes 393248 | tf_op jit(solution)/shard_map/ppermute | solution.py:367
  97.2 0.0 copy-done
  97.2 30.8 %newton_rows.1 = f32[128,128]{1,0:T(8,128)} custom-call(s32[8]{0:T(128)S(1)} %copy-done, f32[8,72,128]{2,1,0:T(8,128)S(1)} %get-tuple-element.8.gathered_ref, f32[768,128]{1,0:T(8,128)S(1)} %reshape.26.mine_ref, f32[768,128]{1,0:T(8,128)S(1)} %collective-permute-done.5.other_ref), custom_call_target="tpu_custom_call" | custom-call | tf_op jit(solution)/shard_map/newton_rows/pallas_call | solution.py:334
  (4 shorter events, 0.2 us)
Async XLA Ops:
  0.0 97.2 %copy-start = (s32[8]{0:T(128)S(1)}, s32[8]{0:T(128)}, u32[]{:S(2)}) copy-start(s32[8]{0:T(128)} %picks_ref.3) | copy-start | bytes 100
  1.5 2.5 %collective-permute-start = (f32[72,128]{1,0:T(8,128)}, f32[72,128]{1,0:T(8,128)S(1)}, u32[]{:S(2)}, u32[]{:S(2)}) collective-permute-start(f32[72,128]{1,0:T(8,128)} %packed_lines.1), channel_id=1, source_target_pairs={{0,1},{1,0},{2,3},{3,2},{4,5},{5,4},{6,7},{7,6},{8,9},{9,8},{10,11... | collective-permute-start | bytes 110600 | tf_op jit(solution)/shard_map/ppermute | solution.py:360
  4.7 4.2 %collective-permute-start.3 = (f32[144,128]{1,0:T(8,128)S(1)}, f32[144,128]{1,0:T(8,128)S(1)}, u32[]{:S(2)}, u32[]{:S(2)}) collective-permute-start(f32[144,128]{1,0:T(8,128)S(1)} %pad_maximum_fusion.near_ref), channel_id=1, source_target_pairs={{0,6},{2,0},{4,2},{6,4},{1,7},{3,1},{5,3},{7,5},{8,14},{10,8},{12,... | collective-permute-start | bytes 221192 | tf_op jit(solution)/shard_map/ppermute | solution.py:361
  7.6 4.8 %collective-permute-start.2 = (f32[144,128]{1,0:T(8,128)S(1)}, f32[144,128]{1,0:T(8,128)S(1)}, u32[]{:S(2)}, u32[]{:S(2)}) collective-permute-start(f32[144,128]{1,0:T(8,128)S(1)} %pad_maximum_fusion.near_ref), channel_id=1, source_target_pairs={{0,4},{2,6},{4,0},{6,2},{1,5},{3,7},{5,1},{7,3},{8,12},{10,14},{12... | collective-permute-start | bytes 221192 | tf_op jit(solution)/shard_map/ppermute | solution.py:361
  7.9 6.5 %collective-permute-start.1 = (f32[144,128]{1,0:T(8,128)S(1)}, f32[144,128]{1,0:T(8,128)S(1)}, u32[]{:S(2)}, u32[]{:S(2)}) collective-permute-start(f32[144,128]{1,0:T(8,128)S(1)} %pad_maximum_fusion.near_ref), channel_id=1, source_target_pairs={{0,2},{2,4},{4,6},{6,0},{1,3},{3,5},{5,7},{7,1},{8,10},{10,12},{12... | collective-permute-start | bytes 221192 | tf_op jit(solution)/shard_map/ppermute | solution.py:361
  53.7 2.3 %collective-permute-start.4 = (f32[768,128]{1,0:T(8,128)S(1)}, f32[768,128]{1,0:T(8,128)S(1)}, u32[]{:S(2)}, u32[]{:S(2)}) collective-permute-start(f32[768,128]{1,0:T(8,128)S(1)} %get-tuple-element.10), channel_id=1, source_target_pairs={{0,1},{1,0},{2,3},{3,2},{4,5},{5,4},{6,7},{7,6},{8,9},{9,8},{10,11... | collective-permute-start | bytes 1179656 | tf_op jit(solution)/shard_map/ppermute | solution.py:363
  92.6 4.7 %collective-permute-start.5 = (f32[768,128]{1,0:T(8,128)S(1)}, f32[768,128]{1,0:T(8,128)S(1)}, u32[]{:S(2)}, u32[]{:S(2)}) collective-permute-start(f32[768,128]{1,0:T(8,128)S(1)} %reshape.26.mine_ref), channel_id=1, source_target_pairs={{0,1},{1,0},{2,3},{3,2},{4,5},{5,4},{6,7},{7,6},{8,9},{9,8},{10,11... | collective-permute-start | bytes 1179656 | tf_op jit(solution)/shard_map/ppermute | solution.py:367

commit v5 on v4

--- a/solution.py
+++ b/solution.py
@@ -55,10 +55,10 @@
     @pl.when(step == 0)
     def _():
         sums_ref[...] = jnp.zeros_like(sums_ref)
-        y, core = lax.axis_index(Y), lax.axis_index(C)
+        y = lax.axis_index(Y)
         for shift, pair_ref in enumerate((near_ref, one_ref, two_ref, three_ref)):
             for j in range(2):
-                source = (y + 4 - shift) % 4 * 2 + (core + j) % 2
+                source = (y + 4 - shift) % 4 * 2 + j
                 gathered_ref[source] = pair_ref[j * LINES : (j + 1) * LINES, :]
         coef_ref[0:NPART, :] = particles(gathered_ref).astype(bf16)
         rows = []
@@ -144,7 +144,7 @@
             out = jnp.where(sub == k, rows[k], out)
         return out
 
-    def panel(p, carry):
+    def panel(p, base):
         first = p * 8
         corner = [[row_of(sys_ref, first + k, first + i) if i >= k else None for k in range(8)] for i in range(8)]
         low = [[None] * 8 for _ in range(8)]
@@ -169,40 +169,44 @@
             for k in range(8):
                 for m in range(k):
                     columns[k] = columns[k] - columns[m] * low[k][m]
-                panel_ref[k, at, :] = columns[k]
+                panel_ref[base + k, at, :] = columns[k]
                 factor = columns[k] * inverse[k]
                 sys_ref[first + k, at, :] = factor
                 for r in range(8):
-                    wide_ref[t * 8 + r, k] = jnp.broadcast_to(factor[r : r + 1], (8, R))
+                    wide_ref[t * 8 + r, base + k] = jnp.broadcast_to(factor[r : r + 1], (8, R))
                 rhs = rhs - factor * y[k]
             rhs_ref[at, :] = rhs
             return carry
 
         lax.fori_loop(p, tiles, below, 0)
 
+    def update(depth, size, tj, start, h, carry):
+        at = [tile_at(start + size * h + e) for e in range(size)]
+        for j in range(8):
+            row = tj * 8 + j
+            total = [sys_ref[row, at[e], :] for e in range(size)]
+            for k in range(depth):
+                factor = wide_ref[row, k]
+                for e in range(size):
+                    total[e] = total[e] - panel_ref[k, at[e], :] * factor
+            for e in range(size):
+                sys_ref[row, at[e], :] = total[e]
+        return carry
+
+    def two_panels(q, carry):
+        p = 2 * q
+        panel(p, 0)
+        lax.fori_loop(p + 1, tiles, functools.partial(update, 8, 1, p + 1, 0), 0)
+        panel(p + 1, 8)
+
         def trailing(tj, carry):
-            def group(size, start, h, carry):
-                at = [tile_at(start + size * h + e) for e in range(size)]
-                columns = [[panel_ref[k, at[e], :] for k in range(8)] for e in range(size)]
-                for j in range(8):
-                    row = tj * 8 + j
-                    total = [None] * size
-                    for k in range(8):
-                        factor = wide_ref[row, k]
-                        for e in range(size):
-                            term = columns[e][k] * factor
-                            total[e] = term if k == 0 else total[e] + term
-                    for e in range(size):
-                        sys_ref[row, at[e], :] = sys_ref[row, at[e], :] - total[e]
-                return carry
-
-            rest = (tiles - tj) % 3
-            lax.fori_loop(0, rest, functools.partial(group, 1, tj), carry)
-            return lax.fori_loop(0, (tiles - tj) // 3, functools.partial(group, 3, tj + rest), carry)
-
-        return lax.fori_loop(p + 1, tiles, trailing, carry)
-
-    lax.fori_loop(0, tiles, panel, 0)
+            odd = (tiles - tj) % 2
+            lax.fori_loop(0, odd, functools.partial(update, 16, 1, tj, tj), carry)
+            return lax.fori_loop(0, (tiles - tj) // 2, functools.partial(update, 16, 2, tj, tj + odd), carry)
+
+        return lax.fori_loop(p + 2, tiles, trailing, carry)
+
+    lax.fori_loop(0, tiles // 2, two_panels, 0)
 
     def back(n, carry):
         p = tiles - 1 - n
@@ -323,7 +327,7 @@
             sys_ref[g * 8 + k, tile_at(g), :] += jnp.where(sub == k, share_sum, 0.0)
         return carry
 
-    lax.fori_loop(0, R // 8, assemble, 0, unroll=4)
+    lax.fori_loop(0, R // 8, assemble, 0, unroll=8)
     factor_and_solve(sys_ref, panel_ref, wide_ref, rhs_ref, step_ref)
     out_ref[...] = jnp.where(valid > 0.5, own + step_ref[...].T, 0.0)
 
@@ -339,8 +343,8 @@
         scratch_shapes=[
             pltpu.VMEM((ROWS, R), f32),
             pltpu.VMEM((R, R, R), f32),
-            pltpu.VMEM((8, R, R), f32),
-            pltpu.VMEM((R, 8, 8, R), f32),
+            pltpu.VMEM((16, R, R), f32),
+            pltpu.VMEM((R, 16, 8, R), f32),
             pltpu.VMEM((R, R), f32),
             pltpu.VMEM((R, R), f32),
         ],
@@ -357,7 +361,7 @@
 def body(coefficients, copies, owner, snapshots, basis, observed, precision):
     swap = [(0, 1), (1, 0)]
     lines = packed_lines(coefficients, copies, owner)
-    pair = jnp.concatenate([lines, lax.ppermute(lines, C, swap)], axis=0)
+    pair = lax.all_gather(lines, C, axis=0, tiled=True)
     pairs = [pair] + [lax.ppermute(pair, Y, [(y, (y + shift) % 4) for y in range(4)]) for shift in (1, 2, 3)]
     gathered, keep, send = points_pass(snapshots, pairs, observed, precision, basis)
     part = keep + lax.ppermute(send, C, swap)

time: 128 us -> 128 us (level)
  blocking collectives: 36.2 us -> 39.3 us
  starting transfers between devices: 9.6 us -> 8.22 us
    all_gather x0 -> x1, blocking collectives: none -> 3.13 us  [body(): pair = lax.all_gather(lines, C, axis=0, tiled=True)]
    ppermute x1 -> x0, starting transfers between devices: 1.42 us -> none  [body(): pair = jnp.concatenate([lines, lax.ppermute(lines, C, swap)], axis=0)]
  transfers between devices with their start and end apart: 6 -> 5, of which waited for: 6 -> 5; matrix products, arithmetic and copies ran while one was open for 0% -> 0% of each run, Pallas kernels for 0% -> 0%
where the time goes in v5:
time: 128 us; the launch traced here: 127 us
  Pallas kernels  71.1 us (56%)
  blocking collectives  39.3 us (31%)
  waiting for transfers between devices  8.46 us (7%)
  starting transfers between devices  8.22 us (6%)
    pallas_call x1, Pallas kernels, points_pass(): pl.pallas_call(functools.partial(points_kernel, block, chunk), out_shape=...  39.3 us
    pallas_call x1, Pallas kernels, newton_rows(): pl.pallas_call(steps_kernel, out_shape=jax.ShapeDtypeStruct((R, R), f32),...  30.3 us
    all_to_all x1, blocking collectives, body(): lax.all_to_all(part.reshape(chips, HALF // chips, R), CHIPS, 0, 0, tiled=...  20.7 us
    all_to_all x1, blocking collectives, sent_to_all(): return lax.all_to_all(copies, axes, split_axis=0, concat_axis=0, tiled=True)  15.5 us
    ppermute x3, waiting for transfers between devices, body(): lax.ppermute(pair, Y, [(y, (y + shift) % 4) for y in range(4)])  5.77 us
    ppermute x3, starting transfers between devices, body(): lax.ppermute(pair, Y, [(y, (y + shift) % 4) for y in range(4)])  3.86 us
    ppermute x1, starting transfers between devices, body(): other = lax.ppermute(mine, C, swap)  3.32 us
    all_gather x1, blocking collectives, body(): pair = lax.all_gather(lines, C, axis=0, tiled=True)  3.13 us
  transfers between devices with their start and end apart: 5, of which 5 were waited for; matrix products, arithmetic and copies ran while one was open for 0% of the time, Pallas kernels for 0%

profile of v5, /device:TPU:1, one launch (start us, length us, event | category | flops | bytes accessed | tf_op | source)
XLA Modules:
  0.0 127.4 jit_solution(16854659399911182181)
XLA Ops:
  0.0 0.0 copy-start
  0.0 1.5 %packed_lines.1 = f32[72,128]{1,0:T(8,128)} custom-call(f32[64,128]{1,0:T(8,128)} %coef_ref.1, s32[1,64]{1,0:T(1,128)} %bitcast.7, s32[1,64]{1,0:T(1,128)} %bitcast.8), custom_call_target="tpu_custom_call" | custom-call | tf_op jit(solution)/shard_map/packed_lines/pallas_call | solution.py:39
  1.5 3.1 %all_gather.3.near_ref = f32[144,128]{1,0:T(8,128)S(1)} all-gather(f32[72,128]{1,0:T(8,128)} %packed_lines.1), channel_id=1, replica_groups=mesh['field_0'=4,'field_1'=4,'dom_0'=4,'dom_1'=2] {'dom_1'}, dimensions={0}, use_global_device_ids=true | all-gather | bytes 110592 | tf_op jit(solution)/shard_map/all_gather | solution.py:364
  4.6 2.8 %collective-permute-start.2 = (f32[144,128]{1,0:T(8,128)S(1)}, f32[144,128]{1,0:T(8,128)S(1)}, u32[]{:S(2)}, u32[]{:S(2)}) collective-permute-start(f32[144,128]{1,0:T(8,128)S(1)} %all_gather.3.near_ref), channel_id=1, source_target_pairs={{0,6},{2,0},{4,2},{6,4},{1,7},{3,1},{5,3},{7,5},{8,14},{10,8},{12,... | collective-permute-start | bytes 221192 | tf_op jit(solution)/shard_map/ppermute | solution.py:365
  7.4 0.3 collective-permute-start.1
  7.8 0.7 collective-permute-start
  8.5 0.4 collective-permute-done.2.three_ref
  8.8 3.4 %collective-permute-done.1.two_ref = f32[144,128]{1,0:T(8,128)S(1)} collective-permute-done((f32[144,128]{1,0:T(8,128)S(1)}, f32[144,128]{1,0:T(8,128)S(1)}, u32[]{:S(2)}, u32[]{:S(2)}) %collective-permute-start.1) | collective-permute-done | bytes 73760 | tf_op jit(solution)/shard_map/ppermute | solution.py:365
  12.2 2.0 %collective-permute-done.one_ref = f32[144,128]{1,0:T(8,128)S(1)} collective-permute-done((f32[144,128]{1,0:T(8,128)S(1)}, f32[144,128]{1,0:T(8,128)S(1)}, u32[]{:S(2)}, u32[]{:S(2)}) %collective-permute-start) | collective-permute-done | bytes 73760 | tf_op jit(solution)/shard_map/ppermute | solution.py:365
  14.2 39.3 %points_pass.1 = (f32[8,72,128]{2,1,0:T(8,128)S(1)}, f32[768,128]{1,0:T(8,128)S(1)}, f32[768,128]{1,0:T(8,128)S(1)}) custom-call(s32[8]{0:T(128)} %picks_ref.3, f32[144,128]{1,0:T(8,128)S(1)} %all_gather.3.near_ref, f32[144,128]{1,0:T(8,128)S(1)} %collective-permute-done.one_ref, f32[144,128]{1,0:T(8,128)S(1)} %collective-permute-done.1.two_ref, ...), custom_call_target="tpu_custom_call" | custom-call | tf_op jit(solution)/shard_map/points_pass/pallas_call | solution.py:105
  53.6 1.0 collective-permute-start.3
  54.6 1.3 %collective-permute-done.3 = f32[768,128]{1,0:T(8,128)S(1)} collective-permute-done((f32[768,128]{1,0:T(8,128)S(1)}, f32[768,128]{1,0:T(8,128)S(1)}, u32[]{:S(2)}, u32[]{:S(2)}) %collective-permute-start.3) | collective-permute-done | bytes 393248 | tf_op jit(solution)/shard_map/ppermute | solution.py:367
  56.0 0.1 add.3
  56.1 20.7 %all_to_all.10 = f32[64,12,128]{2,1,0:T(8,128)S(1)} all-to-all(f32[64,12,128]{2,1,0:T(8,128)S(1)} %reshape.25), channel_id=1, replica_groups=mesh['field_0'=4,'field_1'=4,'dom_0'=4,'dom_1'=2] {'field_0','field_1','..., dimensions={0} | all-to-all | bytes 786432 | tf_op jit(solution)/shard_map/all_to_all | solution.py:369
  76.7 0.1 reduce_sum.9
  76.9 15.5 %all_to_all.11 = f32[64,12,128]{2,1,0:T(8,128)S(1)} all-to-all(f32[64,12,128]{2,1,0:T(8,128)S(1)} %broadcast_in_dim.3), channel_id=1, replica_groups=mesh['field_0'=4,'field_1'=4,'dom_0'=4,'dom_1'=2] {'field_0','field_1','..., dimensions={0} | all-to-all | bytes 786432 | tf_op jit(solution)/shard_map/all_to_all | solution.py:358
  92.4 3.3 %collective-permute-start.4 = (f32[768,128]{1,0:T(8,128)S(1)}, f32[768,128]{1,0:T(8,128)S(1)}, u32[]{:S(2)}, u32[]{:S(2)}) collective-permute-start(f32[768,128]{1,0:T(8,128)S(1)} %reshape.26.mine_ref), channel_id=1, source_target_pairs={{0,1},{1,0},{2,3},{3,2},{4,5},{5,4},{6,7},{7,6},{8,9},{9,8},{10,11... | collective-permute-start | bytes 1179656 | tf_op jit(solution)/shard_map/ppermute | solution.py:371
  95.8 1.3 %collective-permute-done.4.other_ref = f32[768,128]{1,0:T(8,128)S(1)} collective-permute-done((f32[768,128]{1,0:T(8,128)S(1)}, f32[768,128]{1,0:T(8,128)S(1)}, u32[]{:S(2)}, u32[]{:S(2)}) %collective-permute-start.4) | collective-permute-done | bytes 393248 | tf_op jit(solution)/shard_map/ppermute | solution.py:371
  97.1 0.0 copy-done
  97.1 30.3 %newton_rows.1 = f32[128,128]{1,0:T(8,128)} custom-call(s32[8]{0:T(128)S(1)} %copy-done, f32[8,72,128]{2,1,0:T(8,128)S(1)} %get-tuple-element.8.gathered_ref, f32[768,128]{1,0:T(8,128)S(1)} %reshape.26.mine_ref, f32[768,128]{1,0:T(8,128)S(1)} %collective-permute-done.4.other_ref), custom_call_target="tpu_custom_call" | custom-call | tf_op jit(solution)/shard_map/newton_rows/pallas_call | solution.py:338
  (3 shorter events, 0.1 us)
Async XLA Ops:
  0.0 97.1 %copy-start = (s32[8]{0:T(128)S(1)}, s32[8]{0:T(128)}, u32[]{:S(2)}) copy-start(s32[8]{0:T(128)} %picks_ref.3) | copy-start | bytes 100
  4.6 4.2 %collective-permute-start.2 = (f32[144,128]{1,0:T(8,128)S(1)}, f32[144,128]{1,0:T(8,128)S(1)}, u32[]{:S(2)}, u32[]{:S(2)}) collective-permute-start(f32[144,128]{1,0:T(8,128)S(1)} %all_gather.3.near_ref), channel_id=1, source_target_pairs={{0,6},{2,0},{4,2},{6,4},{1,7},{3,1},{5,3},{7,5},{8,14},{10,8},{12,... | collective-permute-start | bytes 221192 | tf_op jit(solution)/shard_map/ppermute | solution.py:365
  7.4 4.8 %collective-permute-start.1 = (f32[144,128]{1,0:T(8,128)S(1)}, f32[144,128]{1,0:T(8,128)S(1)}, u32[]{:S(2)}, u32[]{:S(2)}) collective-permute-start(f32[144,128]{1,0:T(8,128)S(1)} %all_gather.3.near_ref), channel_id=1, source_target_pairs={{0,4},{2,6},{4,0},{6,2},{1,5},{3,7},{5,1},{7,3},{8,12},{10,14},{12... | collective-permute-start | bytes 221192 | tf_op jit(solution)/shard_map/ppermute | solution.py:365
  7.8 6.5 %collective-permute-start = (f32[144,128]{1,0:T(8,128)S(1)}, f32[144,128]{1,0:T(8,128)S(1)}, u32[]{:S(2)}, u32[]{:S(2)}) collective-permute-start(f32[144,128]{1,0:T(8,128)S(1)} %all_gather.3.near_ref), channel_id=1, source_target_pairs={{0,2},{2,4},{4,6},{6,0},{1,3},{3,5},{5,7},{7,1},{8,10},{10,12},{12... | collective-permute-start | bytes 221192 | tf_op jit(solution)/shard_map/ppermute | solution.py:365
  53.6 2.4 %collective-permute-start.3 = (f32[768,128]{1,0:T(8,128)S(1)}, f32[768,128]{1,0:T(8,128)S(1)}, u32[]{:S(2)}, u32[]{:S(2)}) collective-permute-start(f32[768,128]{1,0:T(8,128)S(1)} %get-tuple-element.10), channel_id=1, source_target_pairs={{0,1},{1,0},{2,3},{3,2},{4,5},{5,4},{6,7},{7,6},{8,9},{9,8},{10,11... | collective-permute-start | bytes 1179656 | tf_op jit(solution)/shard_map/ppermute | solution.py:367
  92.4 4.7 %collective-permute-start.4 = (f32[768,128]{1,0:T(8,128)S(1)}, f32[768,128]{1,0:T(8,128)S(1)}, u32[]{:S(2)}, u32[]{:S(2)}) collective-permute-start(f32[768,128]{1,0:T(8,128)S(1)} %reshape.26.mine_ref), channel_id=1, source_target_pairs={{0,1},{1,0},{2,3},{3,2},{4,5},{5,4},{6,7},{7,6},{8,9},{9,8},{10,11... | collective-permute-start | bytes 1179656 | tf_op jit(solution)/shard_map/ppermute | solution.py:371

commit v6 on v5

--- a/solution.py
+++ b/solution.py
@@ -44,12 +44,18 @@
     )(coefficients, copies.reshape(1, NP_DEV), owner.reshape(1, NP_DEV))
 
 
+def in_three(x):
+    high = x.astype(bf16).astype(f32)
+    middle = (x - high).astype(bf16).astype(f32)
+    return high, middle, x - high - middle
+
+
 def particles(gathered_ref):
     return jnp.concatenate([gathered_ref[d, 0:NP_DEV, :] for d in range(N_DOM)], axis=0)
 
 
 def points_kernel(block, chunk, picks_ref, near_ref, one_ref, two_ref, three_ref, obs_ref, prec_ref, basis_ref,
-                  gathered_ref, keep_ref, send_ref, coef_ref, sums_ref, left_ref, right_ref):
+                  gathered_ref, keep_ref, send_ref, coef_ref, pick_ref, sums_ref, left_ref, right_ref):
     step = pl.program_id(0)
 
     @pl.when(step == 0)
@@ -60,28 +66,32 @@
             for j in range(2):
                 source = (y + 4 - shift) % 4 * 2 + j
                 gathered_ref[source] = pair_ref[j * LINES : (j + 1) * LINES, :]
-        coef_ref[0:NPART, :] = particles(gathered_ref).astype(bf16)
+        coef_ref[0:R, :] = particles(gathered_ref).astype(bf16).T
+        minus = lax.broadcasted_iota(jnp.int32, (R, NPART), 0) < 3
+        coef_ref[R : 2 * R, :] = jnp.where(minus, -1.0, 0.0).astype(bf16)
         rows = []
         for s in range(SNAP):
             j = picks_ref[s]
             rows.append(gathered_ref[j // NP_DEV, pl.ds(j % NP_DEV, 1), :])
         rows.append(jnp.zeros((SNAP, R), f32))
-        coef_ref[NPART : NPART + 16, :] = jnp.concatenate(rows, axis=0).astype(bf16)
+        pick_ref[...] = jnp.concatenate(rows, axis=0).astype(bf16)
 
     for c in range(block // chunk):
         at = pl.ds(c * chunk, chunk)
         rows = basis_ref[at, :]
         columns = rows.T
-        prec = prec_ref[:, at]
-        right_ref[at, :] = (columns.astype(f32) * prec).astype(bf16).T
-        field = lax.dot_general(coef_ref[...], rows, last_pair, preferred_element_type=f32)
-        slopes = jnp.tanh(field[: NPART + SNAP] - obs_ref[:, at])
-        left_ref[0:NPART, at] = slopes[:NPART].astype(bf16)
-        picked = slopes[NPART : NPART + SNAP]
-        bend = 1.0 - picked * picked
+        observed = obs_ref[:, at]
+        left_ref[:, at] = (columns.astype(f32) * prec_ref[:, at]).astype(bf16)
+        picked = jnp.dot(pick_ref[...], columns, preferred_element_type=f32)[0:SNAP]
+        slopes = jnp.tanh(picked - observed)
+        bend = (1.0 - slopes * slopes).astype(bf16)
+        terms = jnp.concatenate([*in_three(observed), jnp.zeros((13, chunk), f32)], axis=0).astype(bf16)
+        terms = jnp.concatenate([terms, jnp.zeros((R - 16, chunk), bf16)], axis=0).T
+        field = jnp.dot(jnp.concatenate([rows, terms], axis=1), coef_ref[...], preferred_element_type=f32)
+        right_ref[at, 0:NPART] = jnp.tanh(field).astype(bf16)
         for s in range(SNAP):
-            top = NPART + s * R
-            left_ref[top : top + R, at] = bend[s : s + 1, :].astype(bf16) * columns
+            first = NPART + s * R
+            right_ref[at, first : first + R] = (bend[s : s + 1, :] * columns).T
     sums_ref[...] += jnp.dot(left_ref[...], right_ref[...], preferred_element_type=f32)
 
     @pl.when(step == pl.num_programs(0) - 1)
@@ -90,8 +100,10 @@
 
             @pl.when(lax.axis_index(C) == core)
             def _():
-                keep_ref[...] = sums_ref[core * HALF : (core + 1) * HALF, :]
-                send_ref[...] = sums_ref[(1 - core) * HALF : (2 - core) * HALF, :]
+                for half, part_ref in ((core, keep_ref), (1 - core, send_ref)):
+                    for k in range(HALF // R):
+                        first = half * HALF + k * R
+                        part_ref[k * R : (k + 1) * R, :] = sums_ref[:, first : first + R]
 
 
 def in_hbm(x):
@@ -99,7 +111,7 @@
 
 
 def points_pass(snapshots, pairs, observed, precision, basis):
-    block, chunk = 4096, 512
+    block, chunk = 4096, 256
     count = basis.shape[0]
     whole = lambda i, *_: (0, 0)
     return pl.pallas_call(
@@ -116,10 +128,11 @@
             ],
             out_specs=[pl.BlockSpec((N_DOM, LINES, R), lambda i, *_: (0, 0, 0))] + [pl.BlockSpec((HALF, R), whole)] * 2,
             scratch_shapes=[
-                pltpu.VMEM((NPART + 16, R), bf16),
-                pltpu.VMEM((ROWS, R), f32),
-                pltpu.VMEM((ROWS, block), bf16),
-                pltpu.VMEM((block, R), bf16),
+                pltpu.VMEM((2 * R, NPART), bf16),
+                pltpu.VMEM((16, R), bf16),
+                pltpu.VMEM((R, ROWS), f32),
+                pltpu.VMEM((R, block), bf16),
+                pltpu.VMEM((block, ROWS), bf16),
             ],
         ),
         compiler_params=pltpu.CompilerParams(vmem_limit_bytes=POINTS_VMEM),
@@ -231,12 +244,6 @@
     lax.fori_loop(0, tiles, back, 0)
 
 
-def in_three(x):
-    high = x.astype(bf16).astype(f32)
-    middle = (x - high).astype(bf16).astype(f32)
-    return high, middle, x - high - middle
-
-
 def steps_kernel(picks_ref, gathered_ref, mine_ref, other_ref, out_ref,
                  sums_ref, sys_ref, panel_ref, wide_ref, rhs_ref, step_ref):
     scale = R / PTS
@@ -292,7 +299,11 @@
     low_weights = weights.astype(bf16)
     carried = (everyone + repulse * lifted).astype(bf16)
     numerator = jnp.dot(low_weights, carried, preferred_element_type=f32)
-    grad = jnp.dot(low_weights.astype(f32), sums_ref[0:NPART, :], precision=highest, preferred_element_type=f32)
+    rounded = low_weights.astype(f32)
+    grad = jnp.zeros((R, R), f32)
+    for k in range(0, NPART, R):
+        grad = grad + lax.dot_general(rounded[:, k : k + R], sums_ref[k : k + R, :], last_pair, precision=highest,
+                                      preferred_element_type=f32)
     drift = -(numerator + scale * grad) / total + repulse * own_lift
     rhs_ref[...] = drift.T
 

time: 128 us -> 119 us (0.930)
  Pallas kernels: 71.1 us -> 62.3 us
    pallas_call x1, Pallas kernels: 39.3 us -> 31 us  [points_pass(): pl.pallas_call(functools.partial(points_kernel, block, chunk), out_shape=...]
where the time goes in v6:
time: 119 us
  Pallas kernels  62.3 us (52%)
  blocking collectives  39.3 us (33%)
  waiting for transfers between devices  8.46 us (7%)
  starting transfers between devices  8.22 us (7%)
    pallas_call x1, Pallas kernels, points_pass(): pl.pallas_call(functools.partial(points_kernel, block, chunk), out_shape=...  31 us
    pallas_call x1, Pallas kernels, newton_rows(): pl.pallas_call(steps_kernel, out_shape=jax.ShapeDtypeStruct((R, R), f32),...  29.9 us
    all_to_all x1, blocking collectives, body(): lax.all_to_all(part.reshape(chips, HALF // chips, R), CHIPS, 0, 0, tiled=...  20.7 us
    all_to_all x1, blocking collectives, sent_to_all(): return lax.all_to_all(copies, axes, split_axis=0, concat_axis=0, tiled=True)  15.5 us
    ppermute x3, waiting for transfers between devices, body(): lax.ppermute(pair, Y, [(y, (y + shift) % 4) for y in range(4)])  5.77 us
    ppermute x3, starting transfers between devices, body(): lax.ppermute(pair, Y, [(y, (y + shift) % 4) for y in range(4)])  3.86 us
    ppermute x1, starting transfers between devices, body(): other = lax.ppermute(mine, C, swap)  3.32 us
    all_gather x1, blocking collectives, body(): pair = lax.all_gather(lines, C, axis=0, tiled=True)  3.13 us
  transfers between devices with their start and end apart: 5, of which 5 were waited for; matrix products, arithmetic and copies ran while one was open for 0% of the time, Pallas kernels for 0%

profile of v6, /device:TPU:1, one launch (start us, length us, event | category | flops | bytes accessed | tf_op | source)
XLA Modules:
  0.0 118.6 jit_solution(1880998633015704461)
XLA Ops:
  0.0 0.0 copy-start
  0.0 1.5 %packed_lines.1 = f32[72,128]{1,0:T(8,128)} custom-call(f32[64,128]{1,0:T(8,128)} %coef_ref.1, s32[1,64]{1,0:T(1,128)} %bitcast.7, s32[1,64]{1,0:T(1,128)} %bitcast.8), custom_call_target="tpu_custom_call" | custom-call | tf_op jit(solution)/shard_map/packed_lines/pallas_call | solution.py:39
  1.5 3.1 %all_gather.3.near_ref = f32[144,128]{1,0:T(8,128)S(1)} all-gather(f32[72,128]{1,0:T(8,128)} %packed_lines.1), channel_id=1, replica_groups=mesh['field_0'=4,'field_1'=4,'dom_0'=4,'dom_1'=2] {'dom_1'}, dimensions={0}, use_global_device_ids=true | all-gather | bytes 110592 | tf_op jit(solution)/shard_map/all_gather | solution.py:375
  4.6 2.8 %collective-permute-start.2 = (f32[144,128]{1,0:T(8,128)S(1)}, f32[144,128]{1,0:T(8,128)S(1)}, u32[]{:S(2)}, u32[]{:S(2)}) collective-permute-start(f32[144,128]{1,0:T(8,128)S(1)} %all_gather.3.near_ref), channel_id=1, source_target_pairs={{0,6},{2,0},{4,2},{6,4},{1,7},{3,1},{5,3},{7,5},{8,14},{10,8},{12,... | collective-permute-start | bytes 221192 | tf_op jit(solution)/shard_map/ppermute | solution.py:376
  7.4 0.3 collective-permute-start.1
  7.8 0.7 collective-permute-start
  8.5 0.4 collective-permute-done.2.three_ref
  8.8 3.4 %collective-permute-done.1.two_ref = f32[144,128]{1,0:T(8,128)S(1)} collective-permute-done((f32[144,128]{1,0:T(8,128)S(1)}, f32[144,128]{1,0:T(8,128)S(1)}, u32[]{:S(2)}, u32[]{:S(2)}) %collective-permute-start.1) | collective-permute-done | bytes 73760 | tf_op jit(solution)/shard_map/ppermute | solution.py:376
  12.2 2.0 %collective-permute-done.one_ref = f32[144,128]{1,0:T(8,128)S(1)} collective-permute-done((f32[144,128]{1,0:T(8,128)S(1)}, f32[144,128]{1,0:T(8,128)S(1)}, u32[]{:S(2)}, u32[]{:S(2)}) %collective-permute-start) | collective-permute-done | bytes 73760 | tf_op jit(solution)/shard_map/ppermute | solution.py:376
  14.2 31.0 %points_pass.1 = (f32[8,72,128]{2,1,0:T(8,128)S(1)}, f32[768,128]{1,0:T(8,128)S(1)}, f32[768,128]{1,0:T(8,128)S(1)}) custom-call(s32[8]{0:T(128)} %picks_ref.3, f32[144,128]{1,0:T(8,128)S(1)} %all_gather.3.near_ref, f32[144,128]{1,0:T(8,128)S(1)} %collective-permute-done.one_ref, f32[144,128]{1,0:T(8,128)S(1)} %collective-permute-done.1.two_ref, ...), custom_call_target="tpu_custom_call" | custom-call | tf_op jit(solution)/shard_map/points_pass/pallas_call | solution.py:117
  45.2 1.0 collective-permute-start.3
  46.2 1.3 %collective-permute-done.3 = f32[768,128]{1,0:T(8,128)S(1)} collective-permute-done((f32[768,128]{1,0:T(8,128)S(1)}, f32[768,128]{1,0:T(8,128)S(1)}, u32[]{:S(2)}, u32[]{:S(2)}) %collective-permute-start.3) | collective-permute-done | bytes 393248 | tf_op jit(solution)/shard_map/ppermute | solution.py:378
  47.6 0.1 add.3
  47.7 20.7 %all_to_all.10 = f32[64,12,128]{2,1,0:T(8,128)S(1)} all-to-all(f32[64,12,128]{2,1,0:T(8,128)S(1)} %reshape.25), channel_id=1, replica_groups=mesh['field_0'=4,'field_1'=4,'dom_0'=4,'dom_1'=2] {'field_0','field_1','..., dimensions={0} | all-to-all | bytes 786432 | tf_op jit(solution)/shard_map/all_to_all | solution.py:380
  68.4 0.1 reduce_sum.9
  68.5 15.5 %all_to_all.11 = f32[64,12,128]{2,1,0:T(8,128)S(1)} all-to-all(f32[64,12,128]{2,1,0:T(8,128)S(1)} %broadcast_in_dim.3), channel_id=1, replica_groups=mesh['field_0'=4,'field_1'=4,'dom_0'=4,'dom_1'=2] {'field_0','field_1','..., dimensions={0} | all-to-all | bytes 786432 | tf_op jit(solution)/shard_map/all_to_all | solution.py:369
  84.1 3.3 %collective-permute-start.4 = (f32[768,128]{1,0:T(8,128)S(1)}, f32[768,128]{1,0:T(8,128)S(1)}, u32[]{:S(2)}, u32[]{:S(2)}) collective-permute-start(f32[768,128]{1,0:T(8,128)S(1)} %reshape.26.mine_ref), channel_id=1, source_target_pairs={{0,1},{1,0},{2,3},{3,2},{4,5},{5,4},{6,7},{7,6},{8,9},{9,8},{10,11... | collective-permute-start | bytes 1179656 | tf_op jit(solution)/shard_map/ppermute | solution.py:382
  87.4 1.3 %collective-permute-done.4.other_ref = f32[768,128]{1,0:T(8,128)S(1)} collective-permute-done((f32[768,128]{1,0:T(8,128)S(1)}, f32[768,128]{1,0:T(8,128)S(1)}, u32[]{:S(2)}, u32[]{:S(2)}) %collective-permute-start.4) | collective-permute-done | bytes 393248 | tf_op jit(solution)/shard_map/ppermute | solution.py:382
  88.7 0.0 copy-done
  88.7 29.9 %newton_rows.1 = f32[128,128]{1,0:T(8,128)} custom-call(s32[8]{0:T(128)S(1)} %copy-done, f32[8,72,128]{2,1,0:T(8,128)S(1)} %get-tuple-element.8.gathered_ref, f32[768,128]{1,0:T(8,128)S(1)} %reshape.26.mine_ref, f32[768,128]{1,0:T(8,128)S(1)} %collective-permute-done.4.other_ref), custom_call_target="tpu_custom_call" | custom-call | tf_op jit(solution)/shard_map/newton_rows/pallas_call | solution.py:349
  (3 shorter events, 0.1 us)
Async XLA Ops:
  0.0 88.7 %copy-start = (s32[8]{0:T(128)S(1)}, s32[8]{0:T(128)}, u32[]{:S(2)}) copy-start(s32[8]{0:T(128)} %picks_ref.3) | copy-start | bytes 100
  4.6 4.2 %collective-permute-start.2 = (f32[144,128]{1,0:T(8,128)S(1)}, f32[144,128]{1,0:T(8,128)S(1)}, u32[]{:S(2)}, u32[]{:S(2)}) collective-permute-start(f32[144,128]{1,0:T(8,128)S(1)} %all_gather.3.near_ref), channel_id=1, source_target_pairs={{0,6},{2,0},{4,2},{6,4},{1,7},{3,1},{5,3},{7,5},{8,14},{10,8},{12,... | collective-permute-start | bytes 221192 | tf_op jit(solution)/shard_map/ppermute | solution.py:376
  7.4 4.8 %collective-permute-start.1 = (f32[144,128]{1,0:T(8,128)S(1)}, f32[144,128]{1,0:T(8,128)S(1)}, u32[]{:S(2)}, u32[]{:S(2)}) collective-permute-start(f32[144,128]{1,0:T(8,128)S(1)} %all_gather.3.near_ref), channel_id=1, source_target_pairs={{0,4},{2,6},{4,0},{6,2},{1,5},{3,7},{5,1},{7,3},{8,12},{10,14},{12... | collective-permute-start | bytes 221192 | tf_op jit(solution)/shard_map/ppermute | solution.py:376
  7.8 6.5 %collective-permute-start = (f32[144,128]{1,0:T(8,128)S(1)}, f32[144,128]{1,0:T(8,128)S(1)}, u32[]{:S(2)}, u32[]{:S(2)}) collective-permute-start(f32[144,128]{1,0:T(8,128)S(1)} %all_gather.3.near_ref), channel_id=1, source_target_pairs={{0,2},{2,4},{4,6},{6,0},{1,3},{3,5},{5,7},{7,1},{8,10},{10,12},{12... | collective-permute-start | bytes 221192 | tf_op jit(solution)/shard_map/ppermute | solution.py:376
  45.2 2.4 %collective-permute-start.3 = (f32[768,128]{1,0:T(8,128)S(1)}, f32[768,128]{1,0:T(8,128)S(1)}, u32[]{:S(2)}, u32[]{:S(2)}) collective-permute-start(f32[768,128]{1,0:T(8,128)S(1)} %get-tuple-element.10), channel_id=1, source_target_pairs={{0,1},{1,0},{2,3},{3,2},{4,5},{5,4},{6,7},{7,6},{8,9},{9,8},{10,11... | collective-permute-start | bytes 1179656 | tf_op jit(solution)/shard_map/ppermute | solution.py:378
  84.1 4.7 %collective-permute-start.4 = (f32[768,128]{1,0:T(8,128)S(1)}, f32[768,128]{1,0:T(8,128)S(1)}, u32[]{:S(2)}, u32[]{:S(2)}) collective-permute-start(f32[768,128]{1,0:T(8,128)S(1)} %reshape.26.mine_ref), channel_id=1, source_target_pairs={{0,1},{1,0},{2,3},{3,2},{4,5},{5,4},{6,7},{7,6},{8,9},{9,8},{10,11... | collective-permute-start | bytes 1179656 | tf_op jit(solution)/shard_map/ppermute | solution.py:382

commit v7 on v6

--- a/solution.py
+++ b/solution.py
@@ -352,7 +352,7 @@
         in_specs=[smem, vmem, vmem, vmem],
         out_specs=vmem,
         scratch_shapes=[
-            pltpu.VMEM((ROWS, R), f32),
+            pltpu.VMEM((ROWS + R, R), f32),
             pltpu.VMEM((R, R, R), f32),
             pltpu.VMEM((16, R, R), f32),
             pltpu.VMEM((R, 16, 8, R), f32),

time: 119 us -> 119 us (level)
  no operation moved by 1% of the time
where the time goes in v7:
time: 119 us
  Pallas kernels  62.3 us (52%)
  blocking collectives  39.3 us (33%)
  waiting for transfers between devices  8.46 us (7%)
  starting transfers between devices  8.22 us (7%)
    pallas_call x1, Pallas kernels, points_pass(): pl.pallas_call(functools.partial(points_kernel, block, chunk), out_shape=...  31 us
    pallas_call x1, Pallas kernels, newton_rows(): pl.pallas_call(steps_kernel, out_shape=jax.ShapeDtypeStruct((R, R), f32),...  29.9 us
    all_to_all x1, blocking collectives, body(): lax.all_to_all(part.reshape(chips, HALF // chips, R), CHIPS, 0, 0, tiled=...  20.7 us
    all_to_all x1, blocking collectives, sent_to_all(): return lax.all_to_all(copies, axes, split_axis=0, concat_axis=0, tiled=True)  15.5 us
    ppermute x3, waiting for transfers between devices, body(): lax.ppermute(pair, Y, [(y, (y + shift) % 4) for y in range(4)])  5.77 us
    ppermute x3, starting transfers between devices, body(): lax.ppermute(pair, Y, [(y, (y + shift) % 4) for y in range(4)])  3.86 us
    ppermute x1, starting transfers between devices, body(): other = lax.ppermute(mine, C, swap)  3.32 us
    all_gather x1, blocking collectives, body(): pair = lax.all_gather(lines, C, axis=0, tiled=True)  3.13 us
  transfers between devices with their start and end apart: 5, of which 5 were waited for; matrix products, arithmetic and copies ran while one was open for 0% of the time, Pallas kernels for 0%

profile of v7, /device:TPU:1, one launch (start us, length us, event | category | flops | bytes accessed | tf_op | source)
XLA Modules:
  0.0 118.6 jit_solution(16175851356902450227)
XLA Ops:
  0.0 0.0 copy-start
  0.0 1.5 %packed_lines.1 = f32[72,128]{1,0:T(8,128)} custom-call(f32[64,128]{1,0:T(8,128)} %coef_ref.1, s32[1,64]{1,0:T(1,128)} %bitcast.7, s32[1,64]{1,0:T(1,128)} %bitcast.8), custom_call_target="tpu_custom_call" | custom-call | tf_op jit(solution)/shard_map/packed_lines/pallas_call | solution.py:39
  1.5 3.1 %all_gather.3.near_ref = f32[144,128]{1,0:T(8,128)S(1)} all-gather(f32[72,128]{1,0:T(8,128)} %packed_lines.1), channel_id=1, replica_groups=mesh['field_0'=4,'field_1'=4,'dom_0'=4,'dom_1'=2] {'dom_1'}, dimensions={0}, use_global_device_ids=true | all-gather | bytes 110592 | tf_op jit(solution)/shard_map/all_gather | solution.py:375
  4.6 2.8 %collective-permute-start.2 = (f32[144,128]{1,0:T(8,128)S(1)}, f32[144,128]{1,0:T(8,128)S(1)}, u32[]{:S(2)}, u32[]{:S(2)}) collective-permute-start(f32[144,128]{1,0:T(8,128)S(1)} %all_gather.3.near_ref), channel_id=1, source_target_pairs={{0,6},{2,0},{4,2},{6,4},{1,7},{3,1},{5,3},{7,5},{8,14},{10,8},{12,... | collective-permute-start | bytes 221192 | tf_op jit(solution)/shard_map/ppermute | solution.py:376
  7.4 0.3 collective-permute-start.1
  7.8 0.7 collective-permute-start
  8.5 0.4 collective-permute-done.2.three_ref
  8.8 3.4 %collective-permute-done.1.two_ref = f32[144,128]{1,0:T(8,128)S(1)} collective-permute-done((f32[144,128]{1,0:T(8,128)S(1)}, f32[144,128]{1,0:T(8,128)S(1)}, u32[]{:S(2)}, u32[]{:S(2)}) %collective-permute-start.1) | collective-permute-done | bytes 73760 | tf_op jit(solution)/shard_map/ppermute | solution.py:376
  12.2 2.0 %collective-permute-done.one_ref = f32[144,128]{1,0:T(8,128)S(1)} collective-permute-done((f32[144,128]{1,0:T(8,128)S(1)}, f32[144,128]{1,0:T(8,128)S(1)}, u32[]{:S(2)}, u32[]{:S(2)}) %collective-permute-start) | collective-permute-done | bytes 73760 | tf_op jit(solution)/shard_map/ppermute | solution.py:376
  14.2 31.0 %points_pass.1 = (f32[8,72,128]{2,1,0:T(8,128)S(1)}, f32[768,128]{1,0:T(8,128)S(1)}, f32[768,128]{1,0:T(8,128)S(1)}) custom-call(s32[8]{0:T(128)} %picks_ref.3, f32[144,128]{1,0:T(8,128)S(1)} %all_gather.3.near_ref, f32[144,128]{1,0:T(8,128)S(1)} %collective-permute-done.one_ref, f32[144,128]{1,0:T(8,128)S(1)} %collective-permute-done.1.two_ref, ...), custom_call_target="tpu_custom_call" | custom-call | tf_op jit(solution)/shard_map/points_pass/pallas_call | solution.py:117
  45.2 1.0 collective-permute-start.3
  46.2 1.3 %collective-permute-done.3 = f32[768,128]{1,0:T(8,128)S(1)} collective-permute-done((f32[768,128]{1,0:T(8,128)S(1)}, f32[768,128]{1,0:T(8,128)S(1)}, u32[]{:S(2)}, u32[]{:S(2)}) %collective-permute-start.3) | collective-permute-done | bytes 393248 | tf_op jit(solution)/shard_map/ppermute | solution.py:378
  47.6 0.1 add.3
  47.7 20.7 %all_to_all.10 = f32[64,12,128]{2,1,0:T(8,128)S(1)} all-to-all(f32[64,12,128]{2,1,0:T(8,128)S(1)} %reshape.25), channel_id=1, replica_groups=mesh['field_0'=4,'field_1'=4,'dom_0'=4,'dom_1'=2] {'field_0','field_1','..., dimensions={0} | all-to-all | bytes 786432 | tf_op jit(solution)/shard_map/all_to_all | solution.py:380
  68.4 0.1 reduce_sum.9
  68.5 15.5 %all_to_all.11 = f32[64,12,128]{2,1,0:T(8,128)S(1)} all-to-all(f32[64,12,128]{2,1,0:T(8,128)S(1)} %broadcast_in_dim.3), channel_id=1, replica_groups=mesh['field_0'=4,'field_1'=4,'dom_0'=4,'dom_1'=2] {'field_0','field_1','..., dimensions={0} | all-to-all | bytes 786432 | tf_op jit(solution)/shard_map/all_to_all | solution.py:369
  84.1 3.3 %collective-permute-start.4 = (f32[768,128]{1,0:T(8,128)S(1)}, f32[768,128]{1,0:T(8,128)S(1)}, u32[]{:S(2)}, u32[]{:S(2)}) collective-permute-start(f32[768,128]{1,0:T(8,128)S(1)} %reshape.26.mine_ref), channel_id=1, source_target_pairs={{0,1},{1,0},{2,3},{3,2},{4,5},{5,4},{6,7},{7,6},{8,9},{9,8},{10,11... | collective-permute-start | bytes 1179656 | tf_op jit(solution)/shard_map/ppermute | solution.py:382
  87.4 1.3 %collective-permute-done.4.other_ref = f32[768,128]{1,0:T(8,128)S(1)} collective-permute-done((f32[768,128]{1,0:T(8,128)S(1)}, f32[768,128]{1,0:T(8,128)S(1)}, u32[]{:S(2)}, u32[]{:S(2)}) %collective-permute-start.4) | collective-permute-done | bytes 393248 | tf_op jit(solution)/shard_map/ppermute | solution.py:382
  88.7 0.0 copy-done
  88.7 29.9 %newton_rows.1 = f32[128,128]{1,0:T(8,128)} custom-call(s32[8]{0:T(128)S(1)} %copy-done, f32[8,72,128]{2,1,0:T(8,128)S(1)} %get-tuple-element.8.gathered_ref, f32[768,128]{1,0:T(8,128)S(1)} %reshape.26.mine_ref, f32[768,128]{1,0:T(8,128)S(1)} %collective-permute-done.4.other_ref), custom_call_target="tpu_custom_call" | custom-call | tf_op jit(solution)/shard_map/newton_rows/pallas_call | solution.py:349
  (3 shorter events, 0.1 us)
Async XLA Ops:
  0.0 88.7 %copy-start = (s32[8]{0:T(128)S(1)}, s32[8]{0:T(128)}, u32[]{:S(2)}) copy-start(s32[8]{0:T(128)} %picks_ref.3) | copy-start | bytes 100
  4.6 4.2 %collective-permute-start.2 = (f32[144,128]{1,0:T(8,128)S(1)}, f32[144,128]{1,0:T(8,128)S(1)}, u32[]{:S(2)}, u32[]{:S(2)}) collective-permute-start(f32[144,128]{1,0:T(8,128)S(1)} %all_gather.3.near_ref), channel_id=1, source_target_pairs={{0,6},{2,0},{4,2},{6,4},{1,7},{3,1},{5,3},{7,5},{8,14},{10,8},{12,... | collective-permute-start | bytes 221192 | tf_op jit(solution)/shard_map/ppermute | solution.py:376
  7.4 4.8 %collective-permute-start.1 = (f32[144,128]{1,0:T(8,128)S(1)}, f32[144,128]{1,0:T(8,128)S(1)}, u32[]{:S(2)}, u32[]{:S(2)}) collective-permute-start(f32[144,128]{1,0:T(8,128)S(1)} %all_gather.3.near_ref), channel_id=1, source_target_pairs={{0,4},{2,6},{4,0},{6,2},{1,5},{3,7},{5,1},{7,3},{8,12},{10,14},{12... | collective-permute-start | bytes 221192 | tf_op jit(solution)/shard_map/ppermute | solution.py:376
  7.8 6.5 %collective-permute-start = (f32[144,128]{1,0:T(8,128)S(1)}, f32[144,128]{1,0:T(8,128)S(1)}, u32[]{:S(2)}, u32[]{:S(2)}) collective-permute-start(f32[144,128]{1,0:T(8,128)S(1)} %all_gather.3.near_ref), channel_id=1, source_target_pairs={{0,2},{2,4},{4,6},{6,0},{1,3},{3,5},{5,7},{7,1},{8,10},{10,12},{12... | collective-permute-start | bytes 221192 | tf_op jit(solution)/shard_map/ppermute | solution.py:376
  45.2 2.4 %collective-permute-start.3 = (f32[768,128]{1,0:T(8,128)S(1)}, f32[768,128]{1,0:T(8,128)S(1)}, u32[]{:S(2)}, u32[]{:S(2)}) collective-permute-start(f32[768,128]{1,0:T(8,128)S(1)} %get-tuple-element.10), channel_id=1, source_target_pairs={{0,1},{1,0},{2,3},{3,2},{4,5},{5,4},{6,7},{7,6},{8,9},{9,8},{10,11... | collective-permute-start | bytes 1179656 | tf_op jit(solution)/shard_map/ppermute | solution.py:378
  84.1 4.7 %collective-permute-start.4 = (f32[768,128]{1,0:T(8,128)S(1)}, f32[768,128]{1,0:T(8,128)S(1)}, u32[]{:S(2)}, u32[]{:S(2)}) collective-permute-start(f32[768,128]{1,0:T(8,128)S(1)} %reshape.26.mine_ref), channel_id=1, source_target_pairs={{0,1},{1,0},{2,3},{3,2},{4,5},{5,4},{6,7},{7,6},{8,9},{9,8},{10,11... | collective-permute-start | bytes 1179656 | tf_op jit(solution)/shard_map/ppermute | solution.py:382

commit v8 on v7

--- a/solution.py
+++ b/solution.py
@@ -54,7 +54,7 @@
     return jnp.concatenate([gathered_ref[d, 0:NP_DEV, :] for d in range(N_DOM)], axis=0)
 
 
-def points_kernel(block, chunk, picks_ref, near_ref, one_ref, two_ref, three_ref, obs_ref, prec_ref, basis_ref,
+def points_kernel(block, chunk, picks_ref, near_ref, one_ref, three_ref, two_ref, obs_ref, prec_ref, basis_ref,
                   gathered_ref, keep_ref, send_ref, coef_ref, pick_ref, sums_ref, left_ref, right_ref):
     step = pl.program_id(0)
 
@@ -373,7 +373,7 @@
     swap = [(0, 1), (1, 0)]
     lines = packed_lines(coefficients, copies, owner)
     pair = lax.all_gather(lines, C, axis=0, tiled=True)
-    pairs = [pair] + [lax.ppermute(pair, Y, [(y, (y + shift) % 4) for y in range(4)]) for shift in (1, 2, 3)]
+    pairs = [pair] + [lax.ppermute(pair, Y, [(y, (y + shift) % 4) for y in range(4)]) for shift in (1, 3, 2)]
     gathered, keep, send = points_pass(snapshots, pairs, observed, precision, basis)
     part = keep + lax.ppermute(send, C, swap)
     chips = lax.axis_size(CHIPS)

time: 119 us -> 118 us (level)
  waiting for transfers between devices: 8.46 us -> 6.42 us
  starting transfers between devices: 8.22 us -> 9.95 us
    ppermute x3, waiting for transfers between devices: 5.77 us -> 3.72 us  [body(): lax.ppermute(pair, Y, [(y, (y + shift) % 4) for y in range(4)])]
where the time goes in v8:
time: 118 us
  Pallas kernels  62.3 us (53%)
  blocking collectives  39.2 us (33%)
  starting transfers between devices  9.95 us (8%)
  waiting for transfers between devices  6.42 us (5%)
    pallas_call x1, Pallas kernels, points_pass(): pl.pallas_call(functools.partial(points_kernel, block, chunk), out_shape=...  31 us
    pallas_call x1, Pallas kernels, newton_rows(): pl.pallas_call(steps_kernel, out_shape=jax.ShapeDtypeStruct((R, R), f32),...  29.9 us
    all_to_all x1, blocking collectives, body(): lax.all_to_all(part.reshape(chips, HALF // chips, R), CHIPS, 0, 0, tiled=...  20.5 us
    all_to_all x1, blocking collectives, sent_to_all(): return lax.all_to_all(copies, axes, split_axis=0, concat_axis=0, tiled=True)  15.5 us
    ppermute x3, starting transfers between devices, body(): lax.ppermute(pair, Y, [(y, (y + shift) % 4) for y in range(4)])  4.46 us
    ppermute x3, waiting for transfers between devices, body(): lax.ppermute(pair, Y, [(y, (y + shift) % 4) for y in range(4)])  3.72 us
    ppermute x1, starting transfers between devices, body(): other = lax.ppermute(mine, C, swap)  3.32 us
    all_gather x1, blocking collectives, body(): pair = lax.all_gather(lines, C, axis=0, tiled=True)  3.13 us
  transfers between devices with their start and end apart: 5, of which 5 were waited for; matrix products, arithmetic and copies ran while one was open for 0% of the time, Pallas kernels for 0%

profile of v8, /device:TPU:1, one launch (start us, length us, event | category | flops | bytes accessed | tf_op | source)
XLA Modules:
  0.0 118.1 jit_solution(17113859073886268609)
XLA Ops:
  0.0 0.0 copy-start
  0.0 1.5 %packed_lines.1 = f32[72,128]{1,0:T(8,128)} custom-call(f32[64,128]{1,0:T(8,128)} %coef_ref.1, s32[1,64]{1,0:T(1,128)} %bitcast.7, s32[1,64]{1,0:T(1,128)} %bitcast.8), custom_call_target="tpu_custom_call" | custom-call | tf_op jit(solution)/shard_map/packed_lines/pallas_call | solution.py:39
  1.5 3.1 %all_gather.3.near_ref = f32[144,128]{1,0:T(8,128)S(1)} all-gather(f32[72,128]{1,0:T(8,128)} %packed_lines.1), channel_id=1, replica_groups=mesh['field_0'=4,'field_1'=4,'dom_0'=4,'dom_1'=2] {'dom_1'}, dimensions={0}, use_global_device_ids=true | all-gather | bytes 110592 | tf_op jit(solution)/shard_map/all_gather | solution.py:375
  4.6 3.0 %collective-permute-start.2 = (f32[144,128]{1,0:T(8,128)S(1)}, f32[144,128]{1,0:T(8,128)S(1)}, u32[]{:S(2)}, u32[]{:S(2)}) collective-permute-start(f32[144,128]{1,0:T(8,128)S(1)} %all_gather.3.near_ref), channel_id=1, source_target_pairs={{0,4},{2,6},{4,0},{6,2},{1,5},{3,7},{5,1},{7,3},{8,12},{10,14},{12... | collective-permute-start | bytes 221192 | tf_op jit(solution)/shard_map/ppermute | solution.py:376
  7.6 0.8 collective-permute-start.1
  8.4 0.7 collective-permute-start
  9.1 0.3 collective-permute-done.2.two_ref
  9.3 2.5 %collective-permute-done.1.three_ref = f32[144,128]{1,0:T(8,128)S(1)} collective-permute-done((f32[144,128]{1,0:T(8,128)S(1)}, f32[144,128]{1,0:T(8,128)S(1)}, u32[]{:S(2)}, u32[]{:S(2)}) %collective-permute-start.1) | collective-permute-done | bytes 73760 | tf_op jit(solution)/shard_map/ppermute | solution.py:376
  11.9 0.9 collective-permute-done.one_ref
  12.8 31.0 %points_pass.1 = (f32[8,72,128]{2,1,0:T(8,128)S(1)}, f32[768,128]{1,0:T(8,128)S(1)}, f32[768,128]{1,0:T(8,128)S(1)}) custom-call(s32[8]{0:T(128)} %picks_ref.3, f32[144,128]{1,0:T(8,128)S(1)} %all_gather.3.near_ref, f32[144,128]{1,0:T(8,128)S(1)} %collective-permute-done.one_ref, f32[144,128]{1,0:T(8,128)S(1)} %collective-permute-done.1.three_ref, ...), custom_call_target="tpu_custom_call" | custom-call | tf_op jit(solution)/shard_map/points_pass/pallas_call | solution.py:117
  43.8 2.2 %collective-permute-start.3 = (f32[768,128]{1,0:T(8,128)S(1)}, f32[768,128]{1,0:T(8,128)S(1)}, u32[]{:S(2)}, u32[]{:S(2)}) collective-permute-start(f32[768,128]{1,0:T(8,128)S(1)} %get-tuple-element.10), channel_id=1, source_target_pairs={{0,1},{1,0},{2,3},{3,2},{4,5},{5,4},{6,7},{7,6},{8,9},{9,8},{10,11... | collective-permute-start | bytes 1179656 | tf_op jit(solution)/shard_map/ppermute | solution.py:378
  45.9 1.3 %collective-permute-done.3 = f32[768,128]{1,0:T(8,128)S(1)} collective-permute-done((f32[768,128]{1,0:T(8,128)S(1)}, f32[768,128]{1,0:T(8,128)S(1)}, u32[]{:S(2)}, u32[]{:S(2)}) %collective-permute-start.3) | collective-permute-done | bytes 393248 | tf_op jit(solution)/shard_map/ppermute | solution.py:378
  47.3 0.1 add.3
  47.4 20.5 %all_to_all.10 = f32[64,12,128]{2,1,0:T(8,128)S(1)} all-to-all(f32[64,12,128]{2,1,0:T(8,128)S(1)} %reshape.25), channel_id=1, replica_groups=mesh['field_0'=4,'field_1'=4,'dom_0'=4,'dom_1'=2] {'field_0','field_1','..., dimensions={0} | all-to-all | bytes 786432 | tf_op jit(solution)/shard_map/all_to_all | solution.py:380
  67.9 0.1 reduce_sum.9
  68.0 15.5 %all_to_all.11 = f32[64,12,128]{2,1,0:T(8,128)S(1)} all-to-all(f32[64,12,128]{2,1,0:T(8,128)S(1)} %broadcast_in_dim.3), channel_id=1, replica_groups=mesh['field_0'=4,'field_1'=4,'dom_0'=4,'dom_1'=2] {'field_0','field_1','..., dimensions={0} | all-to-all | bytes 786432 | tf_op jit(solution)/shard_map/all_to_all | solution.py:369
  83.6 3.3 %collective-permute-start.4 = (f32[768,128]{1,0:T(8,128)S(1)}, f32[768,128]{1,0:T(8,128)S(1)}, u32[]{:S(2)}, u32[]{:S(2)}) collective-permute-start(f32[768,128]{1,0:T(8,128)S(1)} %reshape.26.mine_ref), channel_id=1, source_target_pairs={{0,1},{1,0},{2,3},{3,2},{4,5},{5,4},{6,7},{7,6},{8,9},{9,8},{10,11... | collective-permute-start | bytes 1179656 | tf_op jit(solution)/shard_map/ppermute | solution.py:382
  86.9 1.3 %collective-permute-done.4.other_ref = f32[768,128]{1,0:T(8,128)S(1)} collective-permute-done((f32[768,128]{1,0:T(8,128)S(1)}, f32[768,128]{1,0:T(8,128)S(1)}, u32[]{:S(2)}, u32[]{:S(2)}) %collective-permute-start.4) | collective-permute-done | bytes 393248 | tf_op jit(solution)/shard_map/ppermute | solution.py:382
  88.2 0.0 copy-done
  88.2 29.9 %newton_rows.1 = f32[128,128]{1,0:T(8,128)} custom-call(s32[8]{0:T(128)S(1)} %copy-done, f32[8,72,128]{2,1,0:T(8,128)S(1)} %get-tuple-element.8.gathered_ref, f32[768,128]{1,0:T(8,128)S(1)} %reshape.26.mine_ref, f32[768,128]{1,0:T(8,128)S(1)} %collective-permute-done.4.other_ref), custom_call_target="tpu_custom_call" | custom-call | tf_op jit(solution)/shard_map/newton_rows/pallas_call | solution.py:349
  (3 shorter events, 0.1 us)
Async XLA Ops:
  0.0 88.2 %copy-start = (s32[8]{0:T(128)S(1)}, s32[8]{0:T(128)}, u32[]{:S(2)}) copy-start(s32[8]{0:T(128)} %picks_ref.3) | copy-start | bytes 100
  4.6 4.7 %collective-permute-start.2 = (f32[144,128]{1,0:T(8,128)S(1)}, f32[144,128]{1,0:T(8,128)S(1)}, u32[]{:S(2)}, u32[]{:S(2)}) collective-permute-start(f32[144,128]{1,0:T(8,128)S(1)} %all_gather.3.near_ref), channel_id=1, source_target_pairs={{0,4},{2,6},{4,0},{6,2},{1,5},{3,7},{5,1},{7,3},{8,12},{10,14},{12... | collective-permute-start | bytes 221192 | tf_op jit(solution)/shard_map/ppermute | solution.py:376
  7.6 4.3 %collective-permute-start.1 = (f32[144,128]{1,0:T(8,128)S(1)}, f32[144,128]{1,0:T(8,128)S(1)}, u32[]{:S(2)}, u32[]{:S(2)}) collective-permute-start(f32[144,128]{1,0:T(8,128)S(1)} %all_gather.3.near_ref), channel_id=1, source_target_pairs={{0,6},{2,0},{4,2},{6,4},{1,7},{3,1},{5,3},{7,5},{8,14},{10,8},{12,... | collective-permute-start | bytes 221192 | tf_op jit(solution)/shard_map/ppermute | solution.py:376
  8.4 4.4 %collective-permute-start = (f32[144,128]{1,0:T(8,128)S(1)}, f32[144,128]{1,0:T(8,128)S(1)}, u32[]{:S(2)}, u32[]{:S(2)}) collective-permute-start(f32[144,128]{1,0:T(8,128)S(1)} %all_gather.3.near_ref), channel_id=1, source_target_pairs={{0,2},{2,4},{4,6},{6,0},{1,3},{3,5},{5,7},{7,1},{8,10},{10,12},{12... | collective-permute-start | bytes 221192 | tf_op jit(solution)/shard_map/ppermute | solution.py:376
  43.8 3.5 %collective-permute-start.3 = (f32[768,128]{1,0:T(8,128)S(1)}, f32[768,128]{1,0:T(8,128)S(1)}, u32[]{:S(2)}, u32[]{:S(2)}) collective-permute-start(f32[768,128]{1,0:T(8,128)S(1)} %get-tuple-element.10), channel_id=1, source_target_pairs={{0,1},{1,0},{2,3},{3,2},{4,5},{5,4},{6,7},{7,6},{8,9},{9,8},{10,11... | collective-permute-start | bytes 1179656 | tf_op jit(solution)/shard_map/ppermute | solution.py:378
  83.6 4.7 %collective-permute-start.4 = (f32[768,128]{1,0:T(8,128)S(1)}, f32[768,128]{1,0:T(8,128)S(1)}, u32[]{:S(2)}, u32[]{:S(2)}) collective-permute-start(f32[768,128]{1,0:T(8,128)S(1)} %reshape.26.mine_ref), channel_id=1, source_target_pairs={{0,1},{1,0},{2,3},{3,2},{4,5},{5,4},{6,7},{7,6},{8,9},{9,8},{10,11... | collective-permute-start | bytes 1179656 | tf_op jit(solution)/shard_map/ppermute | solution.py:382
